TPU v7x, 256 devices: a whole 4x4x8 slice. The times are simulated.
256 devices in a mesh: section: 4 (over z_hi), ep: 64 (over y, x, z_lo, core).
Axes of the slice: x: 4, y: 4, z: 8 (z_hi: 4, z_lo: 2; z = z_hi * 2 + z_lo), core: 2. Of those that a mesh axis runs over, the one named last changes fastest.
Arguments:
- fresh_tokens: bfloat16 [1024, 3584], P('ep'), may hold values from -6 to 6
- sent_forward: bfloat16 [4, 1024, 3584], P('section', 'ep'), may hold values from -6 to 6
- sent_backward: bfloat16 [4, 1024, 3584], P('section', 'ep'), may hold values from -1.1953125 to 1.1953125
- turn_gradient: bfloat16 [1024, 3584], P('ep'), may hold values from -1.1953125 to 1.1953125
- saved_input: bfloat16 [4, 1024, 3584], P('section', 'ep'), may hold values from -6 to 6
- gain: bfloat16 [4, 3584], P('section'), may hold values from 0.5 to 1.5
- ids_front: int32 [4, 1024, 2], P('section', 'ep'), may hold values from 0 to 7, all different within a row; in each aligned block of 16 rows (0 to 15, 16 to 31, ..., all dimensions but the last counted through in order) at most 8 rows name the same one
- affinity_front: float32 [4, 1024, 2], P('section', 'ep'), may hold values from 0.1 to 1
- ids_back: int32 [4, 1024, 2], P('section', 'ep'), may hold values from 0 to 7, all different within a row; in each aligned block of 16 rows (0 to 15, 16 to 31, ..., all dimensions but the last counted through in order) at most 8 rows name the same one
- affinity_back: float32 [4, 1024, 2], P('section', 'ep'), may hold values from 0.1 to 1
- w_gate: bfloat16 [4, 3584, 8192], P('section', None, 'ep'), may hold values from -0.09375 to 0.09375
- w_up: bfloat16 [4, 3584, 8192], P('section', None, 'ep'), may hold values from -0.09375 to 0.09375
- w_down: bfloat16 [4, 8192, 3584], P('section', 'ep'), may hold values from -0.1875 to 0.1875
- mirror_gate: bfloat16 [4, 3584, 8192], P('section', None, 'ep'), may hold values from -6 to 6
- mirror_up: bfloat16 [4, 3584, 8192], P('section', None, 'ep'), may hold values from -6 to 6
- mirror_down: bfloat16 [4, 8192, 3584], P('section', 'ep'), may hold values from -6 to 6
Outputs:
- forward_out: bfloat16 [4, 1024, 3584], P('section', 'ep')
- grad_input: bfloat16 [4, 1024, 3584], P('section', 'ep')
- grad_gate: bfloat16 [4, 3584, 8192], P('section', None, 'ep')
- grad_up: bfloat16 [4, 3584, 8192], P('section', None, 'ep')
- grad_down: bfloat16 [4, 8192, 3584], P('section', 'ep')
Inputs may be any that keep to these rules, and one draw needn't show every extreme that they name: `ids_front`: each row names 2 different experts. In each aligned block of 16 rows (the rows of one device) no expert is named by more than 8 rows, a bound that some block reaches. `ids_back`: each row names 2 different experts. In each aligned block of 16 rows (the rows of one device) no expert is named by more than 8 rows, a bound that some block reaches.
All inputs are finite; a program needn't handle non-finite values.
Results may differ from a plain program's by a relative error of at most 0.0068.
Values may be sent and summed in bfloat16 or wider, within the bound.
A program may use at most 128 MiB of HBM per device.

v0:
```python
import jax
import jax.numpy as jnp
from jax import lax
from jax.sharding import PartitionSpec as P

EXPERTS = 8


highest = lax.Precision.HIGHEST


def passed_along(value, axis, by):
    peers = lax.axis_size(axis)
    pairs = [(i, i + by) for i in range(peers) if 0 <= i + by < peers]
    return lax.ppermute(value, axis, pairs)


def silu_of(pre_act):
    return pre_act * jax.nn.sigmoid(pre_act)


def norm_rows(inputs, gain):
    values = inputs.astype(jnp.float32)
    inverse = lax.rsqrt(jnp.mean(values * values, axis=-1, keepdims=True) + 1e-06)
    normed = (values * inverse * gain.astype(jnp.float32)).astype(jnp.bfloat16)
    return (values, inverse, normed)


def slot_tables(route_ids, affinity, capacity):
    flat_ids = route_ids.reshape(-1)
    onehot = (flat_ids[:, None] == jnp.arange(EXPERTS, dtype=jnp.int32)[None, :]).astype(jnp.int32)
    earlier = jnp.cumsum(onehot, axis=0) - onehot
    position = jnp.sum(earlier * onehot, axis=1)
    target = (flat_ids * capacity + position).reshape(route_ids.shape)
    columns = jnp.arange(EXPERTS * capacity, dtype=jnp.int32)
    matches = (target[:, :, None] == columns[None, None, :]).astype(jnp.float32)
    shares = affinity / jnp.sum(affinity, axis=1, keepdims=True)
    return (jnp.sum(matches, axis=1), jnp.sum(matches * shares[:, :, None], axis=1))


def to_experts(packed, groups):
    row_width = packed.shape[-1]
    capacity = packed.shape[0] // EXPERTS
    sending = jnp.broadcast_to(
        packed.reshape(EXPERTS, 1, capacity, row_width), (EXPERTS, groups, capacity, row_width)
    )
    gathered = lax.all_to_all(
        sending.reshape(EXPERTS * groups, capacity, row_width),
        "ep",
        split_axis=0,
        concat_axis=0,
        tiled=True,
    )
    return gathered


def from_experts(partial_value, groups):
    sources, capacity, row_width = partial_value.shape
    returned_rows = lax.all_to_all(partial_value, "ep", split_axis=0, concat_axis=0, tiled=True)
    summed = jnp.sum(
        returned_rows.astype(jnp.float32).reshape(EXPERTS, groups, capacity, row_width), axis=1
    )
    return summed.reshape(EXPERTS * capacity, row_width)


def expert_partial(token_rows, gate_cols, up_cols, down_rows):
    gate_pre = jnp.dot(token_rows, gate_cols, preferred_element_type=jnp.float32)
    up_pre = jnp.dot(token_rows, up_cols, preferred_element_type=jnp.float32)
    hidden = (silu_of(gate_pre) * up_pre).astype(jnp.bfloat16)
    return jnp.dot(hidden, down_rows, preferred_element_type=jnp.float32).astype(jnp.bfloat16)


def expert_backward(token_rows, grad_rows, gate_cols, up_cols, down_rows):
    last_dims = (((1,), (1,)), ((), ()))
    first_dims = (((0,), (0,)), ((), ()))
    gate_pre = jnp.dot(token_rows, gate_cols, preferred_element_type=jnp.float32)
    up_pre = jnp.dot(token_rows, up_cols, preferred_element_type=jnp.float32)
    gate_sig = jax.nn.sigmoid(gate_pre)
    active = gate_pre * gate_sig
    hidden = (active * up_pre).astype(jnp.bfloat16)
    grad_hidden = lax.dot_general(
        grad_rows, down_rows, last_dims, preferred_element_type=jnp.float32
    )
    grad_down = lax.dot_general(hidden, grad_rows, first_dims, preferred_element_type=jnp.float32)
    grad_gate_pre = (grad_hidden * up_pre * gate_sig * (1.0 + gate_pre * (1.0 - gate_sig))).astype(
        jnp.bfloat16
    )
    grad_up_pre = (grad_hidden * active).astype(jnp.bfloat16)
    grad_gate = lax.dot_general(
        token_rows, grad_gate_pre, first_dims, preferred_element_type=jnp.float32
    )
    grad_up = lax.dot_general(
        token_rows, grad_up_pre, first_dims, preferred_element_type=jnp.float32
    )
    grad_part = lax.dot_general(
        grad_gate_pre, gate_cols, last_dims, preferred_element_type=jnp.float32
    )
    grad_part = grad_part + lax.dot_general(
        grad_up_pre, up_cols, last_dims, preferred_element_type=jnp.float32
    )
    return (grad_gate, grad_up, grad_down, grad_part.astype(jnp.bfloat16))


def body(
    fresh_tokens,
    sent_forward,
    sent_backward,
    turn_gradient,
    saved_input,
    gain,
    ids_front,
    affinity_front,
    ids_back,
    affinity_back,
    w_gate,
    w_up,
    w_down,
    mirror_gate,
    mirror_up,
    mirror_down,
):
    section_id = lax.axis_index("section")
    last_section = lax.axis_size("section") - 1
    groups = lax.axis_size("ep") // EXPERTS
    tokens = fresh_tokens.shape[0]
    capacity = max(groups, tokens * ids_front.shape[2] * 2 // EXPERTS)
    model_width = fresh_tokens.shape[1]
    arrived = passed_along(sent_forward, "section", 1)
    returned = passed_along(sent_backward, "section", -1)
    front_in = jnp.where(section_id == 0, fresh_tokens, arrived[0])
    upstream_in = jnp.where(section_id == last_section, turn_gradient, returned[0])
    values, inverse, normed = norm_rows(front_in, gain[0])
    member, weighted = slot_tables(ids_front[0], affinity_front[0], capacity)
    packed = jnp.dot(
        member.T.astype(jnp.bfloat16), normed, preferred_element_type=jnp.float32
    ).astype(jnp.bfloat16)
    arrived_rows = to_experts(packed, groups)
    partial_value = expert_partial(
        arrived_rows.reshape(-1, model_width), w_gate[0], w_up[0], w_down[0]
    )
    totals = from_experts(partial_value.reshape(arrived_rows.shape), groups)
    mixed = values + jnp.dot(weighted, totals, precision=highest)
    forward_out = mixed.astype(jnp.bfloat16)[None]
    saved_values, saved_inverse, saved_normed = norm_rows(saved_input[0], gain[0])
    member_back, weighted_back = slot_tables(ids_back[0], affinity_back[0], capacity)
    upstream = upstream_in.astype(jnp.float32)
    packed_rows = jnp.dot(
        member_back.T.astype(jnp.bfloat16), saved_normed, preferred_element_type=jnp.float32
    ).astype(jnp.bfloat16)
    packed_grads = jnp.dot(weighted_back.T, upstream, precision=highest).astype(jnp.bfloat16)
    both_rows = to_experts(jnp.concatenate([packed_rows, packed_grads], axis=1), groups)
    flat_rows = both_rows.reshape(-1, 2 * model_width)
    grad_gate, grad_up, grad_down, grad_part = expert_backward(
        flat_rows[:, :model_width], flat_rows[:, model_width:], w_gate[0], w_up[0], w_down[0]
    )
    slot_grads = from_experts(
        grad_part.reshape(both_rows.shape[0], both_rows.shape[1], model_width), groups
    )
    grad_normed = jnp.dot(member_back, slot_grads, precision=highest)
    scaled = grad_normed * gain[0].astype(jnp.float32)
    cubed = saved_inverse * saved_inverse * saved_inverse
    grad_inputs = (
        upstream
        + saved_inverse * scaled
        - cubed * saved_values * jnp.mean(scaled * saved_values, axis=-1, keepdims=True)
    )
    out_gate = (mirror_gate[0].astype(jnp.float32) + grad_gate).astype(jnp.bfloat16)[None]
    out_up = (mirror_up[0].astype(jnp.float32) + grad_up).astype(jnp.bfloat16)[None]
    out_down = (mirror_down[0].astype(jnp.float32) + grad_down).astype(jnp.bfloat16)[None]
    return (forward_out, grad_inputs.astype(jnp.bfloat16)[None], out_gate, out_up, out_down)


def solution(mesh):
    return jax.shard_map(
        body,
        mesh=mesh,
        in_specs=(
            P("ep", None),
            P("section", "ep", None),
            P("section", "ep", None),
            P("ep", None),
            P("section", "ep", None),
            P("section", None),
            P("section", "ep", None),
            P("section", "ep", None),
            P("section", "ep", None),
            P("section", "ep", None),
            P("section", None, "ep"),
            P("section", None, "ep"),
            P("section", "ep", None),
            P("section", None, "ep"),
            P("section", None, "ep"),
            P("section", "ep", None),
        ),
        out_specs=(
            P("section", "ep", None),
            P("section", "ep", None),
            P("section", None, "ep"),
            P("section", None, "ep"),
            P("section", "ep", None),
        ),
        check_vma=False,
    )
```

profile of v0, /device:TPU:2, one launch (start us, length us, event | category | flops | bytes accessed | tf_op | source)
XLA Modules:
  0.0 303.8 jit_solution(1331402168374911795)
XLA Ops:
  0.6 5.3 %collective-permute-start = (bf16[1,16,3584]{2,1,0:T(8,128)(2,1)}, bf16[1,16,3584]{2,1,0:T(8,128)(2,1)S(1)}, u32[]{:S(2)}, u32[]{:S(2)}) collective-permute-start(bf16[1,16,3584]{2,1,0:T(8,128)(2,1)} %param.17), channel_id=1, source_target_pairs={{0,64},{64,128},{128,192},{1,65},{65,129},{129,193},{2,66},{66,130... | collective-permute-start | bytes 344072 | tf_op jit(solution)/shard_map/ppermute | solution.py:15
  6.0 0.7 reduce_sum.123
  6.7 0.7 bitcast_divide_fusion.1
  7.4 0.8 copy.37
  8.1 0.1 eq.63
  8.2 0.8 convert_reduce_fusion.4
  9.1 0.2 select_reduce_fusion.3
  9.4 0.1 copy.38
  9.5 0.7 bitcast_add_fusion.1
  10.2 0.7 convert_reduce_fusion.3
  10.8 1.1 fusion.51
  11.9 0.3 fusion.8
  12.2 2.1 broadcast_in_dim.19
  14.3 9.7 %all-to-all-start = ((bf16[64,8,3584]{2,1,0:T(8,128)(2,1)}), bf16[64,8,3584]{2,1,0:T(8,128)(2,1)}, u32[]{:S(2)}, u32[]{:S(2)}) async-start(bf16[64,8,3584]{2,1,0:T(8,128)(2,1)} %bitcast.112), calls=%async_computation | async-start | bytes 7340032 | tf_op jit(solution)/shard_map/all_to_all | solution.py:47
  24.0 1.3 collective-permute-start.1
  25.3 0.1 copy.39
  25.4 0.1 eq.71
  25.6 0.2 select_reduce_fusion.1
  25.9 0.1 copy.40
  26.1 0.1 fusion.54
  26.3 0.5 multiply_multiply_fusion
  26.8 0.3 convolution_convert_fusion.2
  27.1 5.0 %collective-permute-done.1 = bf16[1,16,3584]{2,1,0:T(8,128)(2,1)S(1)} collective-permute-done((bf16[1,16,3584]{2,1,0:T(8,128)(2,1)S(1)}, bf16[1,16,3584]{2,1,0:T(8,128)(2,1)S(1)}, u32[]{:S(2)}, u32[]{:S(2)}) %collective-permute-start.1) | collective-permute-done | bytes 114720 | tf_op jit(solution)/shard_map/ppermute | solution.py:15
  32.2 0.6 copy-done.6
  32.8 0.6 convolution_convert_fusion.1
  33.4 40.0 %all-to-all-done = bf16[64,8,3584]{2,1,0:T(8,128)(2,1)} async-done(((bf16[64,8,3584]{2,1,0:T(8,128)(2,1)}), bf16[64,8,3584]{2,1,0:T(8,128)(2,1)}, u32[]{:S(2)}, u32[]{:S(2)}) %all-to-all-start) | async-done | bytes 3670048 | tf_op jit(solution)/shard_map/all_to_all | solution.py:47
  73.4 3.9 %broadcast_in_dim.22 = bf16[8,8,8,7168]{3,2,1,0:T(8,128)(2,1)} broadcast(bf16[8,8,7168]{2,1,0:T(8,128)(2,1)S(1)} %maximum_bitcast_fusion), dimensions={0,2,3} | broadcast | bytes 8257536 | tf_op jit(solution)/shard_map/broadcast_in_dim | solution.py:44
  77.4 10.5 %all-to-all-start.2 = ((bf16[64,8,7168]{2,1,0:T(8,128)(2,1)}), bf16[64,8,7168]{2,1,0:T(8,128)(2,1)}, u32[]{:S(2)}, u32[]{:S(2)}) async-start(bf16[64,8,7168]{2,1,0:T(8,128)(2,1)} %bitcast.111), calls=%async_computation.2 | async-start | bytes 14680064 | tf_op jit(solution)/shard_map/all_to_all | solution.py:47
  87.9 3.2 %fusion.13 = f32[512,128]{1,0:T(8,128)S(1)} fusion(bf16[64,8,3584]{2,1,0:T(8,128)(2,1)} %all-to-all-done, bf16[1,3584,128]{2,1,0:T(8,128)(2,1)S(1)} %copy-done.1), kind=kOutput, calls=%fused_computation.25 | convolution fusion | flops 469762048 | bytes 4849664 | tf_op jit(solution)/shard_map/dot_general | solution.py:67
  91.2 7.8 %fusion = bf16[64,8,3584]{2,1,0:T(8,128)(2,1)} fusion(bf16[1,128,3584]{2,1,0:T(8,128)(2,1)S(1)} %copy-done.3, bf16[64,8,3584]{2,1,0:T(8,128)(2,1)} %all-to-all-done, bf16[1,3584,128]{2,1,0:T(8,128)(2,1)S(1)} %copy-done, f32[512,128]{1,0:T(8,128)S(1)} %fusion.13), kind=kOutput, calls=%fused_computation.4 | convolution fusion | flops 941752320 | bytes 9437184 | tf_op jit(solution)/shard_map/dot_general | solution.py:70
  99.0 79.4 %all-to-all-done.2 = bf16[64,8,7168]{2,1,0:T(8,128)(2,1)} async-done(((bf16[64,8,7168]{2,1,0:T(8,128)(2,1)}), bf16[64,8,7168]{2,1,0:T(8,128)(2,1)}, u32[]{:S(2)}, u32[]{:S(2)}) %all-to-all-start.2) | async-done | bytes 7340064 | tf_op jit(solution)/shard_map/all_to_all | solution.py:47
  178.4 17.0 %all-to-all-start.1 = ((bf16[64,8,3584]{2,1,0:T(8,128)(2,1)}), bf16[64,8,3584]{2,1,0:T(8,128)(2,1)}, u32[]{:S(2)}, u32[]{:S(2)}) async-start(bf16[64,8,3584]{2,1,0:T(8,128)(2,1)} %fusion), calls=%async_computation.1 | async-start | bytes 7340032 | tf_op jit(solution)/shard_map/all_to_all | solution.py:59
  195.4 3.1 %fusion.20 = f32[512,128]{1,0:T(8,128)S(1)} fusion(bf16[512,7168]{1,0:T(8,128)(2,1)} %bitcast.20, bf16[1,3584,128]{2,1,0:T(8,128)(2,1)S(1)} %copy-done.1), kind=kOutput, calls=%fused_computation.32 | convolution fusion | flops 469762048 | bytes 4849664 | tf_op jit(solution)/shard_map/dot_general | solution.py:76
  198.6 3.1 %fusion.22 = f32[512,128]{1,0:T(8,128)S(1)} fusion(bf16[512,7168]{1,0:T(8,128)(2,1)} %bitcast.20, bf16[1,3584,128]{2,1,0:T(8,128)(2,1)S(1)} %copy-done), kind=kOutput, calls=%fused_computation.34 | convolution fusion | flops 469762048 | bytes 4849664 | tf_op jit(solution)/shard_map/dot_general | solution.py:77
  201.7 3.2 %multiply_convert_fusion.1 = (bf16[512,128]{1,0:T(8,128)(2,1)S(1)}, bf16[512,128]{1,0:T(8,128)(2,1)S(1)}) fusion(f32[512,128]{1,0:T(8,128)S(1)} %fusion.20, f32[512,128]{1,0:T(8,128)S(1)} %fusion.22, bf16[1,128,3584]{2,1,0:T(8,128)(2,1)S(1)} %copy-done.3, bf16[512,7168]{1,0:T(8,128)(2,1)} %bitcast.20), kind=kOutput, calls=%fused_computation.57 | convolution fusion | flops 470614016 | bytes 5373952 | tf_op jit(solution)/shard_map/dot_general | solution.py:81
  205.0 1.1 fusion.37
  206.1 3.0 %fusion.1 = bf16[64,8,3584]{2,1,0:T(8,128)(2,1)} fusion(f32[512,3584]{1,0:T(8,128)S(1)} %fusion.37, bf16[512,128]{1,0:T(8,128)(2,1)S(1)} %get-tuple-element.11, bf16[1,3584,128]{2,1,0:T(8,128)(2,1)S(1)} %copy-done), kind=kOutput, calls=%fused_computation.5 | convolution fusion | flops 473432064 | bytes 12058624 | tf_op jit(solution)/shard_map/dot_general | solution.py:98
  209.2 33.7 %all-to-all-done.1 = bf16[64,8,3584]{2,1,0:T(8,128)(2,1)} async-done(((bf16[64,8,3584]{2,1,0:T(8,128)(2,1)}), bf16[64,8,3584]{2,1,0:T(8,128)(2,1)}, u32[]{:S(2)}, u32[]{:S(2)}) %all-to-all-start.1) | async-done | bytes 3670048 | tf_op jit(solution)/shard_map/all_to_all | solution.py:59
  242.9 9.3 %all-to-all-start.3 = ((bf16[64,8,3584]{2,1,0:T(8,128)(2,1)}), bf16[64,8,3584]{2,1,0:T(8,128)(2,1)}, u32[]{:S(2)}, u32[]{:S(2)}) async-start(bf16[64,8,3584]{2,1,0:T(8,128)(2,1)} %fusion.1), calls=%async_computation.3 | async-start | bytes 7340032 | tf_op jit(solution)/shard_map/all_to_all | solution.py:59
  252.2 3.7 %fusion.5 = bf16[1,128,3584]{2,1,0:T(8,128)(2,1)} fusion(bf16[512,7168]{1,0:T(8,128)(2,1)} %bitcast.20, bf16[1,128,3584]{2,1,0:T(8,128)(2,1)S(1)} %copy-done.4, f32[512,128]{1,0:T(8,128)S(1)} %copy-done.11, f32[512,128]{1,0:T(8,128)S(1)} %fusion.20), kind=kOutput, calls=%fused_computation.12 | convolution fusion | flops 471531520 | bytes 6029312 | tf_op jit(solution)/shard_map/dot_general | solution.py:84
  256.0 4.2 %fusion.6 = bf16[1,3584,128]{2,1,0:T(8,128)(2,1)} fusion(bf16[512,128]{1,0:T(8,128)(2,1)S(1)} %copy-done.13, bf16[512,7168]{1,0:T(8,128)(2,1)} %bitcast.20, bf16[1,3584,128]{2,1,0:T(8,128)(2,1)S(1)} %copy-done.22), kind=kOutput, calls=%fused_computation.13 | convolution fusion | flops 471138304 | bytes 5636096 | tf_op jit(solution)/shard_map/dot_general | solution.py:92
  260.2 4.1 %fusion.7 = bf16[1,3584,128]{2,1,0:T(8,128)(2,1)} fusion(bf16[512,128]{1,0:T(8,128)(2,1)S(1)} %get-tuple-element.12, bf16[512,7168]{1,0:T(8,128)(2,1)} %bitcast.20, bf16[1,3584,128]{2,1,0:T(8,128)(2,1)S(1)} %copy-done.23), kind=kOutput, calls=%fused_computation.14 | convolution fusion | flops 471138304 | bytes 5636096 | tf_op jit(solution)/shard_map/dot_general | solution.py:89
  264.4 2.6 convert_reduce_fusion.1
  267.1 1.2 fusion.10
  268.3 31.4 %all-to-all-done.3 = bf16[64,8,3584]{2,1,0:T(8,128)(2,1)} async-done(((bf16[64,8,3584]{2,1,0:T(8,128)(2,1)}), bf16[64,8,3584]{2,1,0:T(8,128)(2,1)}, u32[]{:S(2)}, u32[]{:S(2)}) %all-to-all-start.3) | async-done | bytes 3670048 | tf_op jit(solution)/shard_map/all_to_all | solution.py:59
  299.7 2.6 convert_reduce_fusion
  302.3 0.7 fusion.60
  303.0 0.8 fusion.62
  (63 shorter events, 0.7 us)
Async XLA Ops:
  0.6 90.5 %copy-start = (bf16[1,3584,128]{2,1,0:T(8,128)(2,1)S(1)}, bf16[1,3584,128]{2,1,0:T(8,128)(2,1)}, u32[]{:S(2)}) copy-start(bf16[1,3584,128]{2,1,0:T(8,128)(2,1)} %param.27) | copy-start | bytes 2752516
  0.6 10.2 %collective-permute-start = (bf16[1,16,3584]{2,1,0:T(8,128)(2,1)}, bf16[1,16,3584]{2,1,0:T(8,128)(2,1)S(1)}, u32[]{:S(2)}, u32[]{:S(2)}) collective-permute-start(bf16[1,16,3584]{2,1,0:T(8,128)(2,1)} %param.17), channel_id=1, source_target_pairs={{0,64},{64,128},{128,192},{1,65},{65,129},{129,193},{2,66},{66,130... | collective-permute-start | bytes 344072 | tf_op jit(solution)/shard_map/ppermute | solution.py:15
  9.0 17.8 %copy-start.8 = (f32[3584]{0:T(1024)}, f32[3584]{0:T(1024)S(1)}, u32[]{:S(2)}) copy-start(f32[3584]{0:T(1024)S(1)} %convert_reduce_fusion.4) | copy-start | bytes 43012
  14.3 9.7 %copy-start.24 = (bf16[1,16,3584]{2,1,0:T(8,128)(2,1)S(1)}, bf16[1,16,3584]{2,1,0:T(8,128)(2,1)}, u32[]{:S(2)}) copy-start(bf16[1,16,3584]{2,1,0:T(8,128)(2,1)} %param.18) | copy-start | bytes 344068
  14.3 11.0 %copy-start.18 = (f32[1,16,2]{1,2,0:T(2,128)S(1)}, f32[1,16,2]{1,2,0:T(2,128)}, u32[]{:S(2)}) copy-start(f32[1,16,2]{1,2,0:T(2,128)} %param.25) | copy-start | bytes 388
  14.3 11.1 %copy-start.17 = (s32[1,16,2]{1,2,0:T(2,128)S(1)}, s32[1,16,2]{1,2,0:T(2,128)}, u32[]{:S(2)}) copy-start(s32[1,16,2]{1,2,0:T(2,128)} %param.24) | copy-start | bytes 388
  14.3 11.8 %copy-start.2 = (bf16[1,16,3584]{2,1,0:T(8,128)(2,1)S(1)}, bf16[1,16,3584]{2,1,0:T(8,128)(2,1)}, u32[]{:S(2)}) copy-start(bf16[1,16,3584]{2,1,0:T(8,128)(2,1)} %param.20) | copy-start | bytes 344068
  14.3 18.5 %copy-start.5 = (bf16[16,3584]{1,0:T(8,128)(2,1)S(1)}, bf16[16,3584]{1,0:T(8,128)(2,1)}, u32[]{:S(2)}) copy-start(bf16[16,3584]{1,0:T(8,128)(2,1)} %param.19) | copy-start | bytes 344068
  14.3 59.1 %all-to-all-start = ((bf16[64,8,3584]{2,1,0:T(8,128)(2,1)}), bf16[64,8,3584]{2,1,0:T(8,128)(2,1)}, u32[]{:S(2)}, u32[]{:S(2)}) async-start(bf16[64,8,3584]{2,1,0:T(8,128)(2,1)} %bitcast.112), calls=%async_computation | async-start | bytes 7340032 | tf_op jit(solution)/shard_map/all_to_all | solution.py:47
  24.0 8.2 %collective-permute-start.1 = (bf16[1,16,3584]{2,1,0:T(8,128)(2,1)S(1)}, bf16[1,16,3584]{2,1,0:T(8,128)(2,1)S(1)}, u32[]{:S(2)}, u32[]{:S(2)}) collective-permute-start(bf16[1,16,3584]{2,1,0:T(8,128)(2,1)S(1)} %copy-done.24), channel_id=1, source_target_pairs={{64,0},{128,64},{192,128},{65,1},{129,65},{193,129},{66,2},{130,66... | collective-permute-start | bytes 344072 | tf_op jit(solution)/shard_map/ppermute | solution.py:15
  26.1 6.0 %copy-start.14 = (f32[16,64]{1,0:T(8,128)}, f32[16,64]{1,0:T(8,128)S(1)}, u32[]{:S(2)}) copy-start(f32[16,64]{1,0:T(8,128)S(1)} %get-tuple-element.6) | copy-start | bytes 12292
  26.8 5.4 %copy-start.19 = (f32[16]{0:T(128)}, f32[16]{0:T(128)S(1)}, u32[]{:S(2)}) copy-start(f32[16]{0:T(128)S(1)} %get-tuple-element.14) | copy-start | bytes 196
  32.2 0.6 copy-start.6
  77.4 10.5 %copy-start.1 = (bf16[1,3584,128]{2,1,0:T(8,128)(2,1)S(1)}, bf16[1,3584,128]{2,1,0:T(8,128)(2,1)}, u32[]{:S(2)}) copy-start(bf16[1,3584,128]{2,1,0:T(8,128)(2,1)} %param.26) | copy-start | bytes 2752516
  77.4 101.0 %all-to-all-start.2 = ((bf16[64,8,7168]{2,1,0:T(8,128)(2,1)}), bf16[64,8,7168]{2,1,0:T(8,128)(2,1)}, u32[]{:S(2)}, u32[]{:S(2)}) async-start(bf16[64,8,7168]{2,1,0:T(8,128)(2,1)} %bitcast.111), calls=%async_computation.2 | async-start | bytes 14680064 | tf_op jit(solution)/shard_map/all_to_all | solution.py:47
  87.9 3.3 %copy-start.3 = (bf16[1,128,3584]{2,1,0:T(8,128)(2,1)S(1)}, bf16[1,128,3584]{2,1,0:T(8,128)(2,1)}, u32[]{:S(2)}) copy-start(bf16[1,128,3584]{2,1,0:T(8,128)(2,1)} %param.28) | copy-start | bytes 2752516
  178.4 64.5 %all-to-all-start.1 = ((bf16[64,8,3584]{2,1,0:T(8,128)(2,1)}), bf16[64,8,3584]{2,1,0:T(8,128)(2,1)}, u32[]{:S(2)}, u32[]{:S(2)}) async-start(bf16[64,8,3584]{2,1,0:T(8,128)(2,1)} %fusion), calls=%async_computation.1 | async-start | bytes 7340032 | tf_op jit(solution)/shard_map/all_to_all | solution.py:59
  201.7 3.3 %copy-start.10 = (f32[512,128]{1,0:T(8,128)}, f32[512,128]{1,0:T(8,128)S(1)}, u32[]{:S(2)}) copy-start(f32[512,128]{1,0:T(8,128)S(1)} %fusion.22) | copy-start | bytes 786436
  205.0 1.1 copy-start.12
  209.2 43.0 %copy-start.4 = (bf16[1,128,3584]{2,1,0:T(8,128)(2,1)S(1)}, bf16[1,128,3584]{2,1,0:T(8,128)(2,1)}, u32[]{:S(2)}) copy-start(bf16[1,128,3584]{2,1,0:T(8,128)(2,1)} %param.31) | copy-start | bytes 2752516
  209.2 43.0 %copy-start.11 = (f32[512,128]{1,0:T(8,128)S(1)}, f32[512,128]{1,0:T(8,128)}, u32[]{:S(2)}) copy-start(f32[512,128]{1,0:T(8,128)} %copy-done.10) | copy-start | bytes 786436
  242.9 56.8 %all-to-all-start.3 = ((bf16[64,8,3584]{2,1,0:T(8,128)(2,1)}), bf16[64,8,3584]{2,1,0:T(8,128)(2,1)}, u32[]{:S(2)}, u32[]{:S(2)}) async-start(bf16[64,8,3584]{2,1,0:T(8,128)(2,1)} %fusion.1), calls=%async_computation.3 | async-start | bytes 7340032 | tf_op jit(solution)/shard_map/all_to_all | solution.py:59
  252.2 3.8 %copy-start.13 = (bf16[512,128]{1,0:T(8,128)(2,1)S(1)}, bf16[512,128]{1,0:T(8,128)(2,1)}, u32[]{:S(2)}) copy-start(bf16[512,128]{1,0:T(8,128)(2,1)} %copy-done.12) | copy-start | bytes 393220
  252.2 3.8 %copy-start.22 = (bf16[1,3584,128]{2,1,0:T(8,128)(2,1)S(1)}, bf16[1,3584,128]{2,1,0:T(8,128)(2,1)}, u32[]{:S(2)}) copy-start(bf16[1,3584,128]{2,1,0:T(8,128)(2,1)} %param.30) | copy-start | bytes 2752516
  256.0 4.2 %copy-start.23 = (bf16[1,3584,128]{2,1,0:T(8,128)(2,1)S(1)}, bf16[1,3584,128]{2,1,0:T(8,128)(2,1)}, u32[]{:S(2)}) copy-start(bf16[1,3584,128]{2,1,0:T(8,128)(2,1)} %param.29) | copy-start | bytes 2752516
  264.4 2.7 copy-start.16
  267.0 35.3 %copy-start.9 = (f32[3584]{0:T(1024)S(1)}, f32[3584]{0:T(1024)}, u32[]{:S(2)}) copy-start(f32[3584]{0:T(1024)} %copy-done.8) | copy-start | bytes 43012
  267.0 35.3 %copy-start.15 = (f32[16,64]{1,0:T(8,128)S(1)}, f32[16,64]{1,0:T(8,128)}, u32[]{:S(2)}) copy-start(f32[16,64]{1,0:T(8,128)} %copy-done.14) | copy-start | bytes 12292
  267.0 36.0 %copy-start.7 = (bf16[1,16,3584]{2,1,0:T(8,128)(2,1)S(1)}, bf16[1,16,3584]{2,1,0:T(8,128)(2,1)}, u32[]{:S(2)}) copy-start(bf16[1,16,3584]{2,1,0:T(8,128)(2,1)} %copy-done.6) | copy-start | bytes 344068
  267.0 36.0 %copy-start.20 = (f32[16]{0:T(128)S(1)}, f32[16]{0:T(128)}, u32[]{:S(2)}) copy-start(f32[16]{0:T(128)} %copy-done.19) | copy-start | bytes 196
  267.0 36.0 %copy-start.21 = (f32[16]{0:T(128)S(1)}, f32[16]{0:T(128)}, u32[]{:S(2)}) copy-start(f32[16]{0:T(128)} %get-tuple-element.13) | copy-start | bytes 196
where the time goes:
time: 308 us; the launch traced here: 304 us
  waiting for transfers between devices  189 us (61%)
  starting transfers between devices  53.2 us (17%)
  matrix products  39.9 us (13%)
  other arithmetic  12.1 us (4%)
  local copies, waits for them, and re-layouts  8.11 us (3%)
    all_to_all x2, waiting for transfers between devices, to_experts(): lax.all_to_all(sending.reshape(EXPERTS * groups, capacity, row_width), 'e...  119 us
    all_to_all x2, waiting for transfers between devices, from_experts(): lax.all_to_all(partial_value, 'ep', split_axis=0, concat_axis=0, tiled=True)  65.1 us
    all_to_all x2, starting transfers between devices, from_experts(): lax.all_to_all(partial_value, 'ep', split_axis=0, concat_axis=0, tiled=True)  26.4 us
    all_to_all x2, starting transfers between devices, to_experts(): lax.all_to_all(sending.reshape(EXPERTS * groups, capacity, row_width), 'e...  20.2 us
    dot_general x1, matrix products, expert_partial(): jnp.dot(hidden, down_rows, preferred_element_type=jnp.float32)  7.82 us
    ppermute x2, starting transfers between devices, passed_along(): return lax.ppermute(value, axis, pairs)  6.6 us
  transfers between devices with their start and end apart: 6, of which 5 were waited for; matrix products, arithmetic and copies ran while one was open for 16% of the time, Pallas kernels for 0%

commit v1 on v0

v1 whole, which is shorter than its diff:
```python
import functools
import jax
import jax.numpy as jnp
from jax import lax
from jax.experimental import pallas as pl
from jax.experimental.pallas import tpu as pltpu
from jax.sharding import PartitionSpec as P

BF = jnp.bfloat16
F32 = jnp.float32
MESH = pl.DeviceIdType.MESH
D = 3584
W = D // 2
TOK = 16
HID = 128
EXPERTS = 8
ROWS = 256
ROWS_B, GRADS, FRONT = 0, 1, 2
N_AG = 17
N_RS = 14


def kernel(
    fresh, sent_f, sent_b, turn, saved, gain, ids_f, aff_f, ids_b, aff_b,
    w_gate, w_up, w_down, m_gate, m_up, m_down,
    out_f, out_b, o_gate, o_up, o_down,
    g0, g1, pb, core_in, big_in, small_in, last_in, wgu, wd, mg, mu, md,
    dgu_t, hid_t, came_f, came_b,
    ag_send, ag_recv, rs_send, rs_recv, sec_send, sec_recv, load_sem, save_sem,
):
    sec = lax.axis_index("section")
    ep = lax.axis_index("ep")
    core = lax.rem(ep, 2)
    z = lax.rem(ep // 2, 2)
    x = lax.rem(ep // 4, 4)
    y = ep // 16
    expert = ep // 8

    def at(yy, xx, zz, cc):
        return (sec, ((yy * 4 + xx) * 2 + zz) * 2 + cc)

    def turn4(v, by):
        return lax.rem(v + by, 4)

    dev_z = at(y, x, 1 - z, core)
    dev_c = at(y, x, z, 1 - core)
    dev_y = (at(turn4(y, 1), x, z, core), at(turn4(y, 3), x, z, core))
    dev_x = (at(y, turn4(x, 1), z, core), at(y, turn4(x, 3), z, core))
    dev_s = ((turn4(sec, 1), ep), (turn4(sec, 3), ep))

    loads = [
        pltpu.make_async_copy(w_gate, wgu.at[:, pl.ds(0, HID)], load_sem.at[0]),
        pltpu.make_async_copy(w_up, wgu.at[:, pl.ds(HID, HID)], load_sem.at[1]),
        pltpu.make_async_copy(w_down, wd, load_sem.at[2]),
        pltpu.make_async_copy(m_gate, mg, load_sem.at[3]),
        pltpu.make_async_copy(m_up, mu, load_sem.at[4]),
        pltpu.make_async_copy(m_down, md, load_sem.at[5]),
    ]

    def remote(src, dst, send, recv, dev):
        return pltpu.make_async_remote_copy(
            src_ref=src, dst_ref=dst, send_sem=send, recv_sem=recv,
            device_id=dev, device_id_type=MESH,
        )

    pending = {0: [], 1: [], 2: []}

    def slot(u, s, cc, yy, xx):
        ref = (g0, g1)[s]
        if s == 0 and u == ROWS_B:
            return ref.at[u, cc, yy, xx, :, :, pl.ds(0, W)]
        return ref.at[u, cc, yy, xx]

    def ag(u, s):
        base = (u * 2 + s) * N_AG

        def put(k, ref, dev):
            copy = remote(ref, ref, ag_send.at[base + k], ag_recv.at[base + k], dev)
            copy.start()
            pending[u].append(copy)

        def got(k, ref):
            remote(ref, ref, ag_send.at[base + k], ag_recv.at[base + k], dev_c).wait_recv()

        put(0, slot(u, s, core, y, x).at[z], dev_z)
        yield
        got(0, slot(u, s, core, y, x).at[1 - z])

        def ring(k, blk, me, dev):
            left, right, far = turn4(me, 3), turn4(me, 1), turn4(me, 2)
            put(k, blk(me, 0), dev[0])
            put(k + 2, blk(me, 1), dev[1])
            put(k + 1, blk(me, 1), dev[0])
            put(k + 3, blk(me, 0), dev[1])
            yield
            got(k, blk(left, 0))
            put(k + 4, blk(left, 0), dev[0])
            got(k + 2, blk(right, 1))
            put(k + 5, blk(right, 1), dev[1])
            yield
            got(k + 1, blk(left, 1))
            got(k + 3, blk(right, 0))
            yield 1
            got(k + 4, blk(far, 0))
            got(k + 5, blk(far, 1))

        if s == 0:
            yield from ring(1, lambda i, h: slot(u, s, core, y, i).at[h], x, dev_x)
            whole = lambda i: slot(u, s, core, i, slice(None))
            half = lambda i, h: slot(u, s, core, i, pl.ds(2 * h, 2))
            me, dev = y, dev_y
        else:
            yield from ring(1, lambda i, h: slot(u, s, core, i, x).at[h], y, dev_y)
            whole = lambda i: slot(u, s, core, slice(None), i)
            half = lambda i, h: slot(u, s, core, pl.ds(2 * h, 2), i)
            me, dev = x, dev_x
        gen = ring(7, half, me, dev)
        next(gen)
        put(13, whole(me), dev_c)
        yield
        next(gen)
        yield
        next(gen)
        put(14, whole(turn4(me, 3)), dev_c)
        put(15, whole(turn4(me, 1)), dev_c)
        yield
        for _ in gen:
            pass
        put(16, whole(turn4(me, 2)), dev_c)
        yield
        for k, by in ((13, 0), (14, 3), (15, 1), (16, 2)):
            i = turn4(me, by)
            if s == 0:
                got(k, slot(u, s, 1 - core, i, slice(None)))
            else:
                got(k, slot(u, s, 1 - core, slice(None), i))

    done = []

    def part(u, s, cc, yy, xx):
        if u == 0:
            return pb.at[s, cc, yy, xx]
        if s == 0:
            return g0.at[FRONT, cc, yy, xx, :, :, pl.ds(0, W)]
        return g1.at[FRONT, cc, yy, xx]

    def add_into(dst, srcs, count):
        @pl.loop(0, count)
        def _(i):
            total = dst[i].astype(F32)
            for src in srcs:
                total = total + src[i].astype(F32)
            dst[i] = total.astype(BF)

    def rs(u, s):
        q = u * 2 + s
        base = q * N_RS

        def put(k, src, dst, dev):
            copy = remote(src, dst, rs_send.at[base + k], rs_recv.at[base + k], dev)
            copy.start()
            done.append(copy)

        def got(k, ref):
            remote(ref, ref, rs_send.at[base + k], rs_recv.at[base + k], dev_c).wait_recv()

        every = slice(None)
        put(0, part(u, s, 1 - core, every, every), core_in.at[q], dev_c)
        yield
        got(0, core_in.at[q])

        @pl.loop(0, 4)
        def _(yy):
            for xx in range(4):
                mine = part(u, s, core, yy, xx)
                mine[...] = (
                    mine[...].astype(F32) + core_in[q, yy, xx].astype(F32)
                ).astype(BF)

        def ring(k, blk, buf, me, dev, add):
            left, right, far = turn4(me, 3), turn4(me, 1), turn4(me, 2)
            put(k, blk(far, 0), buf(0, 0), dev[0])
            put(k + 1, blk(far, 1), buf(1, 0), dev[1])
            put(k + 2, blk(right, 1), buf(0, 2), dev[0])
            put(k + 3, blk(left, 0), buf(1, 1), dev[1])
            yield
            got(k, buf(0, 0))
            add(blk(right, 0), [buf(0, 0)])
            put(k + 4, blk(right, 0), buf(0, 1), dev[0])
            got(k + 1, buf(1, 0))
            add(blk(left, 1), [buf(1, 0)])
            put(k + 5, blk(left, 1), buf(1, 2), dev[1])
            yield
            got(k + 2, buf(0, 2))
            got(k + 3, buf(1, 1))
            yield
            got(k + 4, buf(0, 1))
            got(k + 5, buf(1, 2))
            add(blk(me, 0), [buf(0, 1), buf(1, 1)])
            add(blk(me, 1), [buf(0, 2), buf(1, 2)])

        def add_big(dst, srcs):
            @pl.loop(0, 2)
            def _(i):
                for j in range(2):
                    total = dst[i, j].astype(F32)
                    for src in srcs:
                        total = total + src[i, j].astype(F32)
                    dst[i, j] = total.astype(BF)

        def add_small(dst, srcs):
            total = dst[...].astype(F32)
            for src in srcs:
                total = total + src[...].astype(F32)
            dst[...] = total.astype(BF)

        big = lambda d, j: big_in.at[q, d, j]
        small = lambda d, j: small_in.at[q, d, j]
        if s == 0:
            yield from ring(1, lambda i, h: part(u, s, core, i, pl.ds(2 * h, 2)), big, y, dev_y, add_big)
            yield from ring(7, lambda i, h: part(u, s, core, y, i).at[h], small, x, dev_x, add_small)
        else:
            yield from ring(1, lambda i, h: part(u, s, core, pl.ds(2 * h, 2), i), big, x, dev_x, add_big)
            yield from ring(7, lambda i, h: part(u, s, core, i, x).at[h], small, y, dev_y, add_small)
        put(13, part(u, s, core, y, x).at[1 - z], last_in.at[q], dev_z)
        yield
        got(13, last_in.at[q])

    def total_of(u):
        halves = [
            part(u, s, core, y, x)[z].astype(F32) + last_in[u * 2 + s].astype(F32)
            for s in range(2)
        ]
        return jnp.concatenate(halves, axis=1)

    def rinv_of(v):
        return lax.rsqrt(jnp.mean(v * v, axis=-1, keepdims=True) + 1e-6)

    def place(u, value, weights=None):
        g0[u, core, y, x, z, :, pl.ds(0, W)] = value[:, :W]
        g1[u, core, y, x, z] = value[:, W:]
        if weights is not None:
            g0[u, core, y, x, z, :, pl.ds(W, 128)] = weights

    def norm(ref):
        v = ref.astype(F32)
        return (v * rinv_of(v) * gain[...].astype(F32)).astype(BF)

    def weights_of(ids, aff):
        share = aff[...] / jnp.sum(aff[...], axis=1, keepdims=True)
        lane = lax.broadcasted_iota(jnp.int32, (TOK, 128), 1)
        named = ids[...]
        out = jnp.zeros((TOK, 128), F32)
        for k in range(2):
            one = share[:, k : k + 1]
            high = one.astype(BF).astype(F32)
            out = out + jnp.where(lane == named[:, k : k + 1], high, 0.0)
            out = out + jnp.where(lane == named[:, k : k + 1] + EXPERTS, one - high, 0.0)
        return out.astype(BF)

    def chunk_at(i):
        return lax.rem(i // 2 + 1 - core, 2), (i % 2) * 2

    def rows_of(u, i):
        cc, yy = chunk_at(i)
        a = g0[u, cc, pl.ds(yy, 2), :, :, :, pl.ds(0, W)].reshape(ROWS, W)
        b = g1[u, cc, pl.ds(yy, 2)].reshape(ROWS, W)
        return a, b

    def share_of(u, i):
        cc, yy = chunk_at(i)
        aux = g0[u, cc, pl.ds(yy, 2), :, :, :, pl.ds(W, 128)].reshape(ROWS, 128).astype(F32)
        lane = lax.broadcasted_iota(jnp.int32, (ROWS, 128), 1)
        mine = (lane == expert) | (lane == expert + EXPERTS)
        return jnp.sum(jnp.where(mine, aux, 0.0), axis=1, keepdims=True)

    def dot(a, b):
        return jnp.dot(a, b, preferred_element_type=F32)

    def dot_t(a, b):
        return lax.dot_general(a, b, (((1,), (1,)), ((), ())), preferred_element_type=F32)

    def pre_acts(u, i):
        a, b = rows_of(u, i)
        gu = dot(a, wgu[pl.ds(0, W)]) + dot(b, wgu[pl.ds(W, W)])
        return gu[:, :HID], gu[:, HID:]

    TILE = 256

    def front_chunk(i):
        cc, yy = chunk_at(i)
        gate, up = pre_acts(FRONT, i)
        hidden = (gate * jax.nn.sigmoid(gate) * up * share_of(FRONT, i)).astype(BF)
        for s in range(2):
            @pl.loop(0, W // TILE)
            def _(n):
                lo = pl.multiple_of(n * TILE, TILE)
                res = dot(hidden, wd[:, pl.ds(s * W + lo, TILE)])
                (g0, g1)[s][FRONT, cc, pl.ds(yy, 2), :, :, :, pl.ds(lo, TILE)] = (
                    res.astype(BF).reshape(2, 4, 2, TOK, TILE)
                )

    def back_chunk(i):
        cc, yy = chunk_at(i)
        gate, up = pre_acts(ROWS_B, i)
        a, b = rows_of(GRADS, i)
        share = share_of(GRADS, i)
        sig = jax.nn.sigmoid(gate)
        active = gate * sig
        grad_hidden = (dot_t(a, wd[:, pl.ds(0, W)]) + dot_t(b, wd[:, pl.ds(W, W)])) * share
        dgate = grad_hidden * up * sig * (1.0 + gate * (1.0 - sig))
        dup = grad_hidden * active
        scaled = active * up * share
        lo = pl.multiple_of((cc * 2 + i % 2) * ROWS, ROWS)
        dgu_t[pl.ds(0, HID), pl.ds(lo, ROWS)] = dgate.T.astype(BF)
        dgu_t[pl.ds(HID, HID), pl.ds(lo, ROWS)] = dup.T.astype(BF)
        hid_t[:, pl.ds(lo, ROWS)] = scaled.T.astype(BF)
        both = jnp.concatenate([dgate, dup], axis=1).astype(BF)
        for s in range(2):
            @pl.loop(0, W // TILE)
            def _(n):
                lo = pl.multiple_of(n * TILE, TILE)
                res = dot_t(both, wgu[pl.ds(s * W + lo, TILE)])
                pb[s, cc, pl.ds(yy, 2), :, :, :, pl.ds(lo, TILE)] = (
                    res.astype(BF).reshape(2, 4, 2, TOK, TILE)
                )

    def grad_tiles(s, first, last):
        @pl.loop(first, last)
        def _(n):
            lo = pl.multiple_of(n * TILE, TILE)
            g = (g0, g1)[s]
            rows = g[ROWS_B, :, :, :, :, :, pl.ds(lo, TILE)].reshape(1024, TILE)
            here = pl.ds(s * W + lo, TILE)
            res = dot(dgu_t[...], rows)
            mg[here] = (mg[here].astype(F32) + res[:HID].T).astype(BF)
            mu[here] = (mu[here].astype(F32) + res[HID:].T).astype(BF)
            cot = g[GRADS, :, :, :, :, :, pl.ds(lo, TILE)].reshape(1024, TILE)
            md[:, here] = (md[:, here].astype(F32) + dot(hid_t[...], cot)).astype(BF)

    def step(*gens):
        for g in gens:
            next(g, None)

    def finish(*gens):
        for g in gens:
            for _ in g:
                pass

    barrier = pltpu.get_barrier_semaphore()
    for dev in (dev_z, dev_c, *dev_y, *dev_x, *dev_s):
        pl.semaphore_signal(barrier, inc=1, device_id=dev, device_id_type=MESH)
    pl.semaphore_wait(barrier, 8)

    sec_copies = [
        remote(sent_b, came_b, sec_send.at[0], sec_recv.at[0], dev_s[1]),
        remote(sent_f, came_f, sec_send.at[1], sec_recv.at[1], dev_s[0]),
    ]
    for copy in sec_copies:
        copy.start()
    for copy in loads:
        copy.start()
    place(ROWS_B, norm(saved[...]))
    b0, b1 = ag(ROWS_B, 0), ag(ROWS_B, 1)
    step(b0, b1)
    sec_copies[0].wait_recv()
    upstream = jnp.where(sec == 3, turn[...], came_b[...])
    came_b[...] = upstream
    place(GRADS, upstream, weights_of(ids_b, aff_b))
    step(b0, b1)
    c0, c1 = ag(GRADS, 0), ag(GRADS, 1)
    step(b0, b1)
    step(b0, b1)
    step(b0, b1)
    step(c0, c1)
    sec_copies[1].wait_recv()
    front = jnp.where(sec == 0, fresh[...], came_f[...])
    came_f[...] = front
    place(FRONT, norm(front), weights_of(ids_f, aff_f))
    f0, f1 = ag(FRONT, 0), ag(FRONT, 1)
    step(c0, c1)
    step(b0, b1)
    step(c0, c1)
    step(c0, c1)
    step(b0, b1)
    step(c0, c1)
    step(b0, b1)
    step(f0, f1)
    finish(b0, b1)
    step(f0, f1)
    step(c0, c1)
    step(f0, f1)
    step(f0, f1)
    step(c0, c1)
    step(f0, f1)
    step(c0, c1)
    finish(c0, c1)
    for copy in loads[:3]:
        copy.wait()
    r0, r1, q0, q1 = rs(0, 0), rs(0, 1), rs(1, 0), rs(1, 1)
    back_chunk(0)
    step(f0, f1)
    back_chunk(1)
    step(r0, r1, f0, f1)
    back_chunk(2)
    step(f0, f1)
    back_chunk(3)
    finish(f0, f1)
    step(r0, r1)
    for copy in pending[FRONT]:
        copy.wait_send()
    front_chunk(0)
    step(r0, r1)
    front_chunk(1)
    step(q0, q1, r0, r1)
    front_chunk(2)
    front_chunk(3)
    step(r0, r1)
    step(q0, q1)
    step(r0, r1)
    step(r0, r1)
    step(r0, r1)
    step(q0, q1)
    finish(r0, r1)
    for copy in loads[3:]:
        copy.wait()
    grad_tiles(0, 0, 4)
    step(q0, q1)
    grad_tiles(0, 4, 7)
    step(q0, q1)
    grad_tiles(1, 0, 4)
    step(q0, q1)
    grad_tiles(1, 4, 7)
    step(q0, q1)
    saves = [
        pltpu.make_async_copy(mg, o_gate, save_sem.at[0]),
        pltpu.make_async_copy(mu, o_up, save_sem.at[1]),
        pltpu.make_async_copy(md, o_down, save_sem.at[2]),
    ]
    for copy in saves:
        copy.start()

    values = saved[...].astype(F32)
    inverse = rinv_of(values)
    scaled = total_of(0) * gain[...].astype(F32)
    out_b[...] = (
        came_b[...].astype(F32)
        + inverse * scaled
        - inverse * inverse * inverse * values * jnp.mean(scaled * values, axis=-1, keepdims=True)
    ).astype(BF)
    finish(q0, q1)
    out_f[...] = (came_f[...].astype(F32) + total_of(1)).astype(BF)

    for copy in sec_copies:
        copy.wait_send()
    for copy in pending[ROWS_B] + pending[GRADS] + done:
        copy.wait_send()
    for copy in saves:
        copy.wait()


def body(*args):
    (fresh, sent_f, sent_b, turn, saved, gain, ids_f, aff_f, ids_b, aff_b,
     w_gate, w_up, w_down, m_gate, m_up, m_down) = args
    vmem = pl.BlockSpec(memory_space=pltpu.VMEM)
    hbm = pl.BlockSpec(memory_space=pl.ANY)
    sds = jax.ShapeDtypeStruct
    dma = pltpu.SemaphoreType.DMA
    outs = pl.pallas_call(
        kernel,
        out_shape=(
            sds((TOK, D), BF), sds((TOK, D), BF),
            sds((D, HID), BF), sds((D, HID), BF), sds((HID, D), BF),
        ),
        in_specs=[vmem] * 10 + [hbm] * 6,
        out_specs=(vmem, vmem, hbm, hbm, hbm),
        scratch_shapes=[
            pltpu.VMEM((3, 2, 4, 4, 2, TOK, W + 128), BF),
            pltpu.VMEM((3, 2, 4, 4, 2, TOK, W), BF),
            pltpu.VMEM((2, 2, 4, 4, 2, TOK, W), BF),
            pltpu.VMEM((4, 4, 4, 2, TOK, W), BF),
            pltpu.VMEM((4, 2, 3, 2, 2, TOK, W), BF),
            pltpu.VMEM((4, 2, 3, TOK, W), BF),
            pltpu.VMEM((4, TOK, W), BF),
            pltpu.VMEM((D, 2 * HID), BF),
            pltpu.VMEM((HID, D), BF),
            pltpu.VMEM((D, HID), BF),
            pltpu.VMEM((D, HID), BF),
            pltpu.VMEM((HID, D), BF),
            pltpu.VMEM((2 * HID, 1024), BF),
            pltpu.VMEM((HID, 1024), BF),
            pltpu.VMEM((TOK, D), BF),
            pltpu.VMEM((TOK, D), BF),
            dma((6 * N_AG,)), dma((6 * N_AG,)),
            dma((4 * N_RS,)), dma((4 * N_RS,)),
            dma((2,)), dma((2,)), dma((6,)), dma((3,)),
        ],
        compiler_params=pltpu.CompilerParams(
            collective_id=0, has_side_effects=True, vmem_limit_bytes=60 * 2**20
        ),
    )(
        fresh, sent_f[0], sent_b[0], turn, saved[0], gain, ids_f[0], aff_f[0], ids_b[0], aff_b[0],
        w_gate[0], w_up[0], w_down[0], m_gate[0], m_up[0], m_down[0],
    )
    return tuple(o[None] for o in outs)


def solution(mesh):
    rows = P("section", "ep", None)
    cols = P("section", None, "ep")
    return jax.shard_map(
        body,
        mesh=mesh,
        in_specs=(
            P("ep", None), rows, rows, P("ep", None), rows, P("section", None),
            rows, rows, rows, rows, cols, cols, rows, cols, cols, rows,
        ),
        out_specs=(rows, rows, cols, cols, rows),
        check_vma=False,
    )
```

time: 308 us -> 158 us (0.51); the launches traced: 304 us -> 158 us
  waiting for transfers between devices: 189 us -> 0 us
  Pallas kernels: 0 us -> 147 us
  starting transfers between devices: 53.2 us -> 0 us
  matrix products: 39.9 us -> 0 us
  other arithmetic: 12.1 us -> 0 us
    all_to_all x4 -> x0, waiting for transfers between devices: 184 us -> none  [the longest x2 119 us: to_experts(): lax.all_to_all(sending.reshape(EXPERTS * groups, capacity, row_width), 'e...]
    pallas_call x0 -> x1, Pallas kernels: none -> 147 us  [body(): pl.pallas_call(kernel, out_shape=(sds((TOK, D), BF), sds((TOK, D), BF), s...]
    all_to_all x4 -> x0, starting transfers between devices: 46.6 us -> none  [the longest x2 26.4 us: from_experts(): lax.all_to_all(partial_value, 'ep', split_axis=0, concat_axis=0, tiled=True)]
    dot_general x15 -> x0, matrix products: 39.9 us -> none  [the longest x1 7.82 us: expert_partial(): jnp.dot(hidden, down_rows, preferred_element_type=jnp.float32)]
    reduce_sum x10 -> x0, other arithmetic: 8.29 us -> none  [the longest x2 5.26 us: from_experts(): jnp.sum(returned_rows.astype(jnp.float32).reshape(EXPERTS, groups, capaci...]
    ppermute x2 -> x0, starting transfers between devices: 6.6 us -> none  [passed_along(): return lax.ppermute(value, axis, pairs)]
    broadcast_in_dim x2 -> x0, local copies, waits for them, and re-layouts: 5.99 us -> none  [to_experts(): jnp.broadcast_to(packed.reshape(EXPERTS, 1, capacity, row_width), (EXPERT...]
    unnamed x52 -> x19, local copies, waits for them, and re-layouts: 1.61 us -> 7.6 us
  transfers between devices with their start and end apart: 6 -> 0, of which waited for: 5 -> 0; matrix products, arithmetic and copies ran while one was open for 16% -> 0% of each run, Pallas kernels for 0% -> 0%
where the time goes in v1:
time: 158 us
  Pallas kernels  147 us (93%)
  local copies, waits for them, and re-layouts  10.3 us (7%)
    pallas_call x1, Pallas kernels, body(): pl.pallas_call(kernel, out_shape=(sds((TOK, D), BF), sds((TOK, D), BF), s...  147 us
    unnamed x19, local copies, waits for them, and re-layouts  7.6 us

profile of v1, /device:TPU:2, one launch (start us, length us, event | category | flops | bytes accessed | tf_op | source)
XLA Modules:
  0.0 157.7 jit_solution(3817512243754691609)
XLA Ops:
  0.6 0.0 copy-start.3
  0.6 0.7 copy-done.3
  1.3 0.0 copy-start.4
  1.3 0.7 copy.21.ids_f
  2.0 0.0 copy-done.4
  2.0 0.0 copy-start.5
  2.0 0.7 copy.22.aff_f
  2.7 0.0 copy-done.5
  2.7 0.0 copy-start.6
  2.7 0.7 copy.23.ids_b
  3.4 0.0 copy-done.6
  3.4 0.7 copy.24.aff_b
  4.0 146.7 %shard_map.191 = (bf16[16,3584]{1,0:T(8,128)(2,1)}, bf16[16,3584]{1,0:T(8,128)(2,1)}, bf16[3584,128]{1,0:T(8,128)(2,1)}, bf16[3584,128]{1,0:T(8,128)(2,1)}, bf16[128,3584]{1,0:T(8,128)(2,1)}) custom-call(bf16[16,3584]{1,0:T(8,128)(2,1)} %fresh.1, bf16[16,3584]{1,0:T(8,128)(2,1)} %bitcast.29, bf16[16,3584]{1,0:T(8,128)(2,1)} %bitcast.30, ...), custom_call_target="tpu_custom_call" | custom-call | tf_op jit(solution)/shard_map/pallas_call | solution.py:469
  150.7 0.0 copy-start.2
  150.7 1.6 %copy.30 = bf16[1,16,3584]{2,1,0:T(8,128)(2,1)} copy(bf16[1,16,3584]{2,1,0:T(8,128)(2,1)} %bitcast.28) | data formatting | bytes 229376
  152.3 0.0 copy-done.2
  152.3 0.6 copy.31
  153.0 0.0 copy-start.1
  153.0 2.2 %copy.32 = bf16[1,3584,128]{2,1,0:T(8,128)(2,1)} copy(bf16[1,3584,128]{2,1,0:T(8,128)(2,1)} %bitcast.26) | data formatting | bytes 1835008
  155.2 0.0 copy-done.1
  155.2 0.0 copy-start
  155.2 0.9 copy.33
  156.1 0.6 copy-done
  156.7 0.9 copy.34
Async XLA Ops:
  0.6 0.7 copy-start.3
  1.3 0.7 copy-start.4
  2.0 0.7 copy-start.5
  2.7 0.7 copy-start.6
  150.7 1.6 %copy-start.2 = (bf16[16,3584]{1,0:T(8,128)(2,1)S(1)}, bf16[16,3584]{1,0:T(8,128)(2,1)}, u32[]{:S(2)}) copy-start(bf16[16,3584]{1,0:T(8,128)(2,1)} %get-tuple-element.11) | copy-start | bytes 344068
  153.0 2.2 %copy-start.1 = (bf16[3584,128]{1,0:T(8,128)(2,1)S(1)}, bf16[3584,128]{1,0:T(8,128)(2,1)}, u32[]{:S(2)}) copy-start(bf16[3584,128]{1,0:T(8,128)(2,1)} %get-tuple-element.13) | copy-start | bytes 2752516
  155.2 1.5 copy-start

commit v2 on v1

v2 whole, which is shorter than its diff:
```python
import functools
import jax
import jax.numpy as jnp
from jax import lax
from jax.experimental import pallas as pl
from jax.experimental.pallas import tpu as pltpu
from jax.sharding import PartitionSpec as P

BF = jnp.bfloat16
F32 = jnp.float32
MESH = pl.DeviceIdType.MESH
D = 3584
W = D // 2
TOK = 16
HID = 128
EXPERTS = 8
ROWS = 256
TILE = 256
CAP = 8
ROWS_B, GRADS, FRONT = 0, 1, 2
N_AG = 17
N_RS = 14


def kernel(
    fresh, sent_f, sent_b, turn, saved, gain, ids_f, aff_f, ids_b, aff_b,
    w_gate, w_up, w_down, m_gate, m_up, m_down,
    out_f, out_b, o_gate, o_up, o_down,
    tk, g0, g1, packed_y, packed_x, relay, part, core_in, slots_y, relay_back, slots_x,
    tokens, small_in, last_in, pick_y, pick_x, pick_y_t, pick_x_t,
    wgu, wd, mg, mu, md, dgu_t, hid_t, came_f, came_b,
    ag_send, ag_recv, rs_send, rs_recv, sec_send, sec_recv, load_sem, save_sem,
):
    sec = lax.axis_index("section")
    ep = lax.axis_index("ep")
    core = lax.rem(ep, 2)
    z = lax.rem(ep // 2, 2)
    x = lax.rem(ep // 4, 4)
    y = ep // 16
    expert = ep // 8
    pair = x // 2
    x_in = x + 1 - 2 * lax.rem(x, 2)

    def at(yy, xx, zz, cc):
        return (sec, ((yy * 4 + xx) * 2 + zz) * 2 + cc)

    def turn4(v, by):
        return lax.rem(v + by, 4)

    dev_z = at(y, x, 1 - z, core)
    dev_c = at(y, x, z, 1 - core)
    dev_y = (at(turn4(y, 1), x, z, core), at(turn4(y, 3), x, z, core))
    dev_x = (at(y, turn4(x, 1), z, core), at(y, turn4(x, 3), z, core))
    x_out = turn4(x, 3 + 2 * lax.rem(x, 2))
    x_far = turn4(x, 2)
    dev_in, dev_out = at(y, x_in, z, core), at(y, x_out, z, core)
    dev_s = ((turn4(sec, 1), ep), (turn4(sec, 3), ep))

    loads = [
        pltpu.make_async_copy(w_gate, wgu.at[:, pl.ds(0, HID)], load_sem.at[0]),
        pltpu.make_async_copy(w_up, wgu.at[:, pl.ds(HID, HID)], load_sem.at[1]),
        pltpu.make_async_copy(w_down, wd, load_sem.at[2]),
        pltpu.make_async_copy(m_gate, mg, load_sem.at[3]),
        pltpu.make_async_copy(m_up, mu, load_sem.at[4]),
        pltpu.make_async_copy(m_down, md, load_sem.at[5]),
    ]

    def remote(src, dst, send, recv, dev):
        return pltpu.make_async_remote_copy(
            src_ref=src, dst_ref=dst, send_sem=send, recv_sem=recv,
            device_id=dev, device_id_type=MESH,
        )

    every = slice(None)
    lane128 = lax.broadcasted_iota(jnp.int32, (128, 128), 1)
    row128 = lax.broadcasted_iota(jnp.int32, (128, 128), 0)
    route_of = (0, 0, 1)
    width_of = (W + 128, W, W + 128)

    def build_picks(u, s):
        route = route_of[u]
        aux = tk[s, u, :, :, :, pl.ds(W, 128)].reshape(128, 128)
        named = jnp.where((aux.astype(F32) > 0.0) & (lane128 < EXPERTS), 1.0, 0.0)
        before = jnp.where((row128 // TOK == lane128 // TOK) & (lane128 < row128), 1.0, 0.0)
        order = dot(before.astype(BF), named.astype(BF))
        block = lax.broadcasted_iota(jnp.int32, (128, 1), 0) // TOK

        def places(e):
            chosen = jnp.sum(jnp.where(lane128 == e, named, 0.0), axis=1, keepdims=True)
            slot = jnp.sum(jnp.where(lane128 == e, order, 0.0), axis=1, keepdims=True)
            return chosen, block * CAP + slot.astype(jnp.int32)

        if s == 0:
            wanted = [2 * turn4(y, r) + pair for r in range(4)]
        else:
            wanted = [2 * y + pair, 2 * y + 1 - pair]
        lane = lax.broadcasted_iota(jnp.int32, (128, 64 * len(wanted)), 1)
        pick = jnp.zeros((128, 64 * len(wanted)), F32)
        for r, e in enumerate(wanted):
            chosen, target = places(e)
            pick = pick + jnp.where(lane == target + 64 * r, chosen, 0.0)
        (pick_y, pick_x)[s][route] = pick.astype(BF)
        (pick_y_t, pick_x_t)[s][route] = pick.T.astype(BF)

    def pack(u, s):
        route = route_of[u]
        if u != GRADS:
            build_picks(u, s)

        def tile(lo, size):
            rows = tk[s, u, :, :, :, pl.ds(lo, size)].reshape(128, size)
            res = dot((pick_y_t, pick_x_t)[s][route], rows).astype(BF)
            if s == 0:
                g0[u, core, y, :, :, pl.ds(lo, size)] = res[:64].reshape(4, TOK, size)
                for r in range(3):
                    packed_y[u, r, :, :, pl.ds(lo, size)] = (
                        res[64 * (r + 1) : 64 * (r + 2)].reshape(4, TOK, size)
                    )
            else:
                g1[u, core, :, x, :, pl.ds(lo, size)] = res[:64].reshape(4, TOK, size)
                packed_x[u, :, :, pl.ds(lo, size)] = res[64:].reshape(4, TOK, size)

        @pl.loop(0, W // TILE)
        def _(n):
            tile(pl.multiple_of(n * TILE, TILE), TILE)

        if s == 0 and u != GRADS:
            tile(W, 128)

    pending = []

    def ag(u, s):
        base = (u * 2 + s) * N_AG

        def put(k, src, dst, dev):
            copy = remote(src, dst, ag_send.at[base + k], ag_recv.at[base + k], dev)
            copy.start()
            pending.append(copy)

        def got(k, ref):
            remote(ref, ref, ag_send.at[base + k], ag_recv.at[base + k], dev_c).wait_recv()

        me, dev = ((x, dev_x), (y, dev_y))[s]

        def blk(i, h):
            return tk.at[s, u, i, h, :, pl.ds(0, width_of[u])]

        def same(k, ref, to):
            put(k, ref, ref, to)

        same(0, blk(me, z), dev_z)
        yield
        got(0, blk(me, 1 - z))
        left, right, far = turn4(me, 3), turn4(me, 1), turn4(me, 2)
        same(1, blk(me, 0), dev[0])
        same(3, blk(me, 1), dev[1])
        same(2, blk(me, 1), dev[0])
        same(4, blk(me, 0), dev[1])
        yield
        got(1, blk(left, 0))
        same(5, blk(left, 0), dev[0])
        got(3, blk(right, 1))
        same(6, blk(right, 1), dev[1])
        yield
        got(2, blk(left, 1))
        got(4, blk(right, 0))
        yield
        got(5, blk(far, 0))
        got(6, blk(far, 1))
        pack(u, s)
        if s == 0:
            wide = pl.ds(0, width_of[u])

            def home(cc, yy, xx):
                return g0.at[u, cc, yy, xx, :, wide]

            low, high = pl.ds(0, 2), pl.ds(2, 2)
            up, down, over = turn4(y, 1), turn4(y, 3), turn4(y, 2)
            put(7, packed_y.at[u, 1, low, :, wide], relay.at[u, 0, :, :, wide], dev_y[0])
            put(8, packed_y.at[u, 1, high, :, wide], relay.at[u, 1, :, :, wide], dev_y[1])
            put(9, packed_y.at[u, 0, :, :, wide], home(core, y, every), dev_y[0])
            put(10, packed_y.at[u, 2, :, :, wide], home(core, y, every), dev_y[1])
            same(13, home(core, y, every), dev_c)
            yield
            got(7, relay.at[u, 0, :, :, wide])
            put(11, relay.at[u, 0, :, :, wide], home(core, down, low), dev_y[0])
            got(8, relay.at[u, 1, :, :, wide])
            put(12, relay.at[u, 1, :, :, wide], home(core, up, high), dev_y[1])
            yield
            got(9, home(core, down, every))
            same(14, home(core, down, every), dev_c)
            got(10, home(core, up, every))
            same(15, home(core, up, every), dev_c)
            yield
            got(11, home(core, over, low))
            got(12, home(core, over, high))
            same(16, home(core, over, every), dev_c)
            yield
            for k, i in ((13, y), (14, down), (15, up), (16, over)):
                got(k, home(1 - core, i, every))
        else:

            def home(cc, yy, xx):
                return g1.at[u, cc, yy, xx]

            low, high = pl.ds(0, 2), pl.ds(2, 2)
            put(7, packed_x.at[u, low], home(core, low, x), dev_out)
            same(9, home(core, every, x), dev_in)
            put(8, packed_x.at[u, high], home(core, high, x), dev_out)
            same(13, home(core, every, x), dev_c)
            yield
            got(7, home(core, low, x_out))
            same(10, home(core, low, x_out), dev_in)
            yield
            got(8, home(core, high, x_out))
            same(11, home(core, high, x_out), dev_in)
            same(14, home(core, every, x_out), dev_c)
            got(9, home(core, every, x_in))
            same(15, home(core, every, x_in), dev_c)
            yield
            got(10, home(core, low, x_far))
            got(11, home(core, high, x_far))
            same(16, home(core, every, x_far), dev_c)
            yield
            for k, i in ((13, x), (14, x_out), (15, x_in), (16, x_far)):
                got(k, home(1 - core, every, i))

    done = []

    def add_into(dst, *srcs):
        total = dst[...].astype(F32)
        for src in srcs:
            total = total + src[...].astype(F32)
        dst[...] = total.astype(BF)

    def rs(u, s):
        q = u * 2 + s
        base = q * N_RS

        def put(k, src, dst, dev):
            copy = remote(src, dst, rs_send.at[base + k], rs_recv.at[base + k], dev)
            copy.start()
            done.append(copy)

        def got(k, ref):
            remote(ref, ref, rs_send.at[base + k], rs_recv.at[base + k], dev_c).wait_recv()

        put(0, part.at[u, s, 1 - core], core_in.at[q], dev_c)
        yield
        got(0, core_in.at[q])

        @pl.loop(0, 4)
        def _(yy):
            for xx in range(4):
                add_into(part.at[u, s, core, yy, xx], core_in.at[q, yy, xx])

        if s == 0:
            low, high = pl.ds(0, 2), pl.ds(2, 2)
            up, down, over = turn4(y, 1), turn4(y, 3), turn4(y, 2)
            put(1, part.at[u, s, core, over, low], relay_back.at[u, 0], dev_y[0])
            put(2, part.at[u, s, core, over, high], relay_back.at[u, 1], dev_y[1])
            put(3, part.at[u, s, core, up], slots_y.at[u, 2], dev_y[0])
            put(4, part.at[u, s, core, down], slots_y.at[u, 0], dev_y[1])
            yield
            got(1, relay_back.at[u, 0])
            put(5, relay_back.at[u, 0], slots_y.at[u, 1, low], dev_y[0])
            got(2, relay_back.at[u, 1])
            put(6, relay_back.at[u, 1], slots_y.at[u, 1, high], dev_y[1])
            yield
            got(3, slots_y.at[u, 2])
            got(4, slots_y.at[u, 0])
            yield
            got(5, slots_y.at[u, 1, low])
            got(6, slots_y.at[u, 1, high])
        else:
            put(1, part.at[u, s, core, :, x_far], slots_x.at[u, 0], dev_in)
            put(2, part.at[u, s, core, :, x_in], slots_x.at[u, 1], dev_in)
            yield
            got(1, slots_x.at[u, 0])
            add_each(part.at[u, s, core, :, x_out], slots_x.at[u, 0])
            put(3, part.at[u, s, core, :, x_out], slots_x.at[u, 2], dev_out)
            yield
            got(2, slots_x.at[u, 1])
            add_each(part.at[u, s, core, :, x], slots_x.at[u, 1])
            yield
            got(3, slots_x.at[u, 2])

        @pl.loop(0, W // TILE)
        def _(n):
            here = pl.ds(pl.multiple_of(n * TILE, TILE), TILE)
            if s == 0:
                pick = pick_y[u]
                rows = [part[u, s, core, y, :, :, here].reshape(64, TILE)] + [
                    slots_y[u, r, :, :, here].reshape(64, TILE) for r in range(3)
                ]
            else:
                pick = pick_x[u]
                rows = [
                    part[u, s, core, :, x, :, here].reshape(64, TILE),
                    slots_x[u, 2, :, :, here].reshape(64, TILE),
                ]
            res = dot(pick, jnp.concatenate(rows, axis=0)).astype(BF)
            tokens[q, :, :, :, here] = res.reshape(4, 2, TOK, TILE)

        me, dev = ((x, dev_x), (y, dev_y))[s]
        left, right, far = turn4(me, 3), turn4(me, 1), turn4(me, 2)

        def blk(i, h):
            return tokens.at[q, i, h]

        def buf(d, j):
            return small_in.at[q, d, j]

        put(7, blk(far, 0), buf(0, 0), dev[0])
        put(8, blk(far, 1), buf(1, 0), dev[1])
        put(9, blk(right, 1), buf(0, 2), dev[0])
        put(10, blk(left, 0), buf(1, 1), dev[1])
        yield
        got(7, buf(0, 0))
        add_into(blk(right, 0), buf(0, 0))
        put(11, blk(right, 0), buf(0, 1), dev[0])
        got(8, buf(1, 0))
        add_into(blk(left, 1), buf(1, 0))
        put(12, blk(left, 1), buf(1, 2), dev[1])
        yield
        got(9, buf(0, 2))
        got(10, buf(1, 1))
        yield
        got(11, buf(0, 1))
        got(12, buf(1, 2))
        add_into(blk(me, 0), buf(0, 1), buf(1, 1))
        add_into(blk(me, 1), buf(0, 2), buf(1, 2))
        put(13, blk(me, 1 - z), last_in.at[q], dev_z)
        yield
        got(13, last_in.at[q])

    def add_each(dst, src):
        for i in range(4):
            add_into(dst.at[i], src.at[i])

    def total_of(u):
        halves = [
            tokens[u * 2 + s, (x, y)[s], z].astype(F32) + last_in[u * 2 + s].astype(F32)
            for s in range(2)
        ]
        return jnp.concatenate(halves, axis=1)

    def rinv_of(v):
        return lax.rsqrt(jnp.mean(v * v, axis=-1, keepdims=True) + 1e-6)

    def place(u, value, weights=None):
        tk[0, u, x, z, :, pl.ds(0, W)] = value[:, :W]
        tk[1, u, y, z, :, pl.ds(0, W)] = value[:, W:]
        if weights is not None:
            tk[0, u, x, z, :, pl.ds(W, 128)] = weights
            tk[1, u, y, z, :, pl.ds(W, 128)] = weights

    def norm(ref):
        v = ref.astype(F32)
        return (v * rinv_of(v) * gain[...].astype(F32)).astype(BF)

    def weights_of(ids, aff):
        lane = lax.broadcasted_iota(jnp.int32, (TOK, 128), 1)
        eye = lax.broadcasted_iota(jnp.int32, (TOK, TOK), 0) == lax.broadcasted_iota(
            jnp.int32, (TOK, TOK), 1
        )

        def column(row):
            wide = jnp.broadcast_to(row.astype(F32), (TOK, TOK))
            return jnp.sum(jnp.where(eye, wide, 0.0), axis=1, keepdims=True)

        named = [column(ids[k : k + 1, :]).astype(jnp.int32) for k in range(2)]
        both = [column(aff[k : k + 1, :]) for k in range(2)]
        out = jnp.zeros((TOK, 128), F32)
        for k in range(2):
            one = both[k] / (both[0] + both[1])
            high = one.astype(BF).astype(F32)
            out = out + jnp.where(lane == named[k], high, 0.0)
            out = out + jnp.where(lane == named[k] + EXPERTS, one - high, 0.0)
        return out.astype(BF)

    def rows_of(u, cc):
        a = g0[u, cc, :, :, :, pl.ds(0, W)].reshape(ROWS, W)
        b = g1[u, cc].reshape(ROWS, W)
        return a, b

    def share_of(u, cc):
        aux = g0[u, cc, :, :, :, pl.ds(W, 128)].reshape(ROWS, 128).astype(F32)
        lane = lax.broadcasted_iota(jnp.int32, (ROWS, 128), 1)
        mine = (lane == expert) | (lane == expert + EXPERTS)
        return jnp.sum(jnp.where(mine, aux, 0.0), axis=1, keepdims=True)

    def dot(a, b):
        return jnp.dot(a, b, preferred_element_type=F32)

    def dot_t(a, b):
        return lax.dot_general(a, b, (((1,), (1,)), ((), ())), preferred_element_type=F32)

    def pre_acts(u, i):
        a, b = rows_of(u, i)
        gu = dot(a, wgu[pl.ds(0, W)]) + dot(b, wgu[pl.ds(W, W)])
        return gu[:, :HID], gu[:, HID:]

    def front_chunk(i):
        cc = (1 - core, core)[i]
        gate, up = pre_acts(FRONT, cc)
        hidden = (gate * jax.nn.sigmoid(gate) * up * share_of(FRONT, cc)).astype(BF)
        for s in range(2):
            @pl.loop(0, W // TILE)
            def _(n):
                lo = pl.multiple_of(n * TILE, TILE)
                res = dot(hidden, wd[:, pl.ds(s * W + lo, TILE)])
                part[1, s, cc, :, :, :, pl.ds(lo, TILE)] = res.astype(BF).reshape(4, 4, TOK, TILE)

    def back_chunk(i):
        cc = (1 - core, core)[i]
        gate, up = pre_acts(ROWS_B, cc)
        a, b = rows_of(GRADS, cc)
        share = share_of(ROWS_B, cc)
        sig = jax.nn.sigmoid(gate)
        active = gate * sig
        grad_hidden = (dot_t(a, wd[:, pl.ds(0, W)]) + dot_t(b, wd[:, pl.ds(W, W)])) * share
        dgate = grad_hidden * up * sig * (1.0 + gate * (1.0 - sig))
        dup = grad_hidden * active
        scaled = active * up * share
        lo = pl.multiple_of(cc * ROWS, ROWS)
        dgu_t[pl.ds(0, HID), pl.ds(lo, ROWS)] = dgate.T.astype(BF)
        dgu_t[pl.ds(HID, HID), pl.ds(lo, ROWS)] = dup.T.astype(BF)
        hid_t[:, pl.ds(lo, ROWS)] = scaled.T.astype(BF)
        both = jnp.concatenate([dgate, dup], axis=1).astype(BF)
        for s in range(2):
            @pl.loop(0, W // TILE)
            def _(n):
                lo = pl.multiple_of(n * TILE, TILE)
                res = dot_t(both, wgu[pl.ds(s * W + lo, TILE)])
                part[0, s, cc, :, :, :, pl.ds(lo, TILE)] = res.astype(BF).reshape(4, 4, TOK, TILE)

    def grad_tiles(s, first, last):
        @pl.loop(first, last)
        def _(n):
            lo = pl.multiple_of(n * TILE, TILE)
            g = (g0, g1)[s]
            rows = g[ROWS_B, :, :, :, :, pl.ds(lo, TILE)].reshape(2 * ROWS, TILE)
            here = pl.ds(s * W + lo, TILE)
            res = dot(dgu_t[...], rows)
            mg[here] = (mg[here].astype(F32) + res[:HID].T).astype(BF)
            mu[here] = (mu[here].astype(F32) + res[HID:].T).astype(BF)
            cot = g[GRADS, :, :, :, :, pl.ds(lo, TILE)].reshape(2 * ROWS, TILE)
            md[:, here] = (md[:, here].astype(F32) + dot(hid_t[...], cot)).astype(BF)

    def step(*gens):
        for g in gens:
            next(g, None)

    def finish(*gens):
        for g in gens:
            for _ in g:
                pass

    barrier = pltpu.get_barrier_semaphore()
    for dev in (dev_z, dev_c, *dev_y, *dev_x, *dev_s):
        pl.semaphore_signal(barrier, inc=1, device_id=dev, device_id_type=MESH)
    pl.semaphore_wait(barrier, 8)

    sec_copies = [
        remote(sent_b, came_b, sec_send.at[0], sec_recv.at[0], dev_s[1]),
        remote(sent_f, came_f, sec_send.at[1], sec_recv.at[1], dev_s[0]),
    ]
    for copy in sec_copies:
        copy.start()
    weights_b = weights_of(ids_b, aff_b)
    place(ROWS_B, norm(saved[...]), weights_b)
    b = ag(ROWS_B, 0), ag(ROWS_B, 1)
    c = ag(GRADS, 0), ag(GRADS, 1)
    f = ag(FRONT, 0), ag(FRONT, 1)
    r = rs(0, 0), rs(0, 1)
    q = rs(1, 0), rs(1, 1)
    step(*b)
    for copy in loads:
        copy.start()
    step(*b)
    weights_f = weights_of(ids_f, aff_f)
    step(*b)
    step(*b)
    step(*b)
    sec_copies[0].wait_recv()
    upstream = jnp.where(sec == 3, turn[...], came_b[...])
    came_b[...] = upstream
    place(GRADS, upstream)
    step(*c)
    sec_copies[1].wait_recv()
    front = jnp.where(sec == 0, fresh[...], came_f[...])
    came_f[...] = front
    place(FRONT, norm(front), weights_f)
    step(*b)
    step(*c)
    step(*c)
    step(*b)
    step(*c)
    step(*c)
    step(*f)
    step(*b)
    step(*f)
    step(*c)
    step(*f)
    step(*c)
    step(*f)
    step(*f)
    step(*c)
    finish(*b)
    finish(*c)
    for copy in loads[:3]:
        copy.wait()
    step(*f)
    back_chunk(0)
    step(*f, *r)
    back_chunk(1)
    finish(*f)
    step(*r)
    front_chunk(0)
    step(*q, *r)
    front_chunk(1)
    step(*r)
    step(*q)
    step(*r)
    step(*r)
    step(*r)
    step(*q)
    finish(*r)
    for copy in loads[3:]:
        copy.wait()
    grad_tiles(0, 0, 7)
    step(*q)
    grad_tiles(1, 0, 7)
    step(*q)
    step(*q)
    step(*q)
    step(*q)
    saves = [
        pltpu.make_async_copy(mg, o_gate, save_sem.at[0]),
        pltpu.make_async_copy(mu, o_up, save_sem.at[1]),
        pltpu.make_async_copy(md, o_down, save_sem.at[2]),
    ]
    for copy in saves:
        copy.start()

    values = saved[...].astype(F32)
    inverse = rinv_of(values)
    scaled = total_of(0) * gain[...].astype(F32)
    out_b[...] = (
        came_b[...].astype(F32)
        + inverse * scaled
        - inverse * inverse * inverse * values * jnp.mean(scaled * values, axis=-1, keepdims=True)
    ).astype(BF)
    finish(*q)
    out_f[...] = (came_f[...].astype(F32) + total_of(1)).astype(BF)

    for copy in sec_copies:
        copy.wait_send()
    for copy in pending + done:
        copy.wait_send()
    for copy in saves:
        copy.wait()


def hand_over(*refs):
    held, came, went = refs[10:15], refs[15], refs[16]
    order = (2, 3, 4, 0, 1)
    ins = {i: pltpu.make_async_copy(refs[i], held[i], came.at[i]) for i in order}
    outs = {i: pltpu.make_async_copy(held[i], refs[5 + i].at[0], went.at[i]) for i in order}
    for i in order:
        ins[i].start()
    for i in order:
        ins[i].wait()
        outs[i].start()
    for i in order:
        outs[i].wait()


def body(*args):
    (fresh, sent_f, sent_b, turn, saved, gain, ids_f, aff_f, ids_b, aff_b,
     w_gate, w_up, w_down, m_gate, m_up, m_down) = args
    vmem = pl.BlockSpec(memory_space=pltpu.VMEM)
    hbm = pl.BlockSpec(memory_space=pl.ANY)
    sds = jax.ShapeDtypeStruct
    dma = pltpu.SemaphoreType.DMA
    outs = pl.pallas_call(
        kernel,
        out_shape=(
            sds((TOK, D), BF), sds((TOK, D), BF),
            sds((D, HID), BF), sds((D, HID), BF), sds((HID, D), BF),
        ),
        in_specs=[vmem] * 10 + [hbm] * 6,
        out_specs=(vmem, vmem, hbm, hbm, hbm),
        scratch_shapes=[
            pltpu.VMEM((2, 3, 4, 2, TOK, W + 128), BF),
            pltpu.VMEM((3, 2, 4, 4, TOK, W + 128), BF),
            pltpu.VMEM((3, 2, 4, 4, TOK, W), BF),
            pltpu.VMEM((3, 3, 4, TOK, W + 128), BF),
            pltpu.VMEM((3, 4, TOK, W), BF),
            pltpu.VMEM((3, 2, 2, TOK, W + 128), BF),
            pltpu.VMEM((2, 2, 2, 4, 4, TOK, W), BF),
            pltpu.VMEM((4, 4, 4, TOK, W), BF),
            pltpu.VMEM((2, 3, 4, TOK, W), BF),
            pltpu.VMEM((2, 2, 2, TOK, W), BF),
            pltpu.VMEM((2, 3, 4, TOK, W), BF),
            pltpu.VMEM((4, 4, 2, TOK, W), BF),
            pltpu.VMEM((4, 2, 3, TOK, W), BF),
            pltpu.VMEM((4, TOK, W), BF),
            pltpu.VMEM((2, 128, 256), BF),
            pltpu.VMEM((2, 128, 128), BF),
            pltpu.VMEM((2, 256, 128), BF),
            pltpu.VMEM((2, 128, 128), BF),
            pltpu.VMEM((D, 2 * HID), BF),
            pltpu.VMEM((HID, D), BF),
            pltpu.VMEM((D, HID), BF),
            pltpu.VMEM((D, HID), BF),
            pltpu.VMEM((HID, D), BF),
            pltpu.VMEM((2 * HID, 2 * ROWS), BF),
            pltpu.VMEM((HID, 2 * ROWS), BF),
            pltpu.VMEM((TOK, D), BF),
            pltpu.VMEM((TOK, D), BF),
            dma((6 * N_AG,)), dma((6 * N_AG,)),
            dma((4 * N_RS,)), dma((4 * N_RS,)),
            dma((2,)), dma((2,)), dma((6,)), dma((3,)),
        ],
        compiler_params=pltpu.CompilerParams(
            collective_id=0, has_side_effects=True, vmem_limit_bytes=60 * 2**20
        ),
    )(
        fresh, sent_f[0], sent_b[0], turn, saved[0], gain, ids_f[0].T, aff_f[0].T, ids_b[0].T, aff_b[0].T,
        w_gate[0], w_up[0], w_down[0], m_gate[0], m_up[0], m_down[0],
    )
    return pl.pallas_call(
        hand_over,
        out_shape=tuple(sds((1, *o.shape), BF) for o in outs),
        in_specs=[hbm] * 5,
        out_specs=(hbm,) * 5,
        scratch_shapes=[*(pltpu.VMEM(o.shape, BF) for o in outs), dma((5,)), dma((5,))],
    )(*outs)


def solution(mesh):
    rows = P("section", "ep", None)
    cols = P("section", None, "ep")
    return jax.shard_map(
        body,
        mesh=mesh,
        in_specs=(
            P("ep", None), rows, rows, P("ep", None), rows, P("section", None),
            rows, rows, rows, rows, cols, cols, rows, cols, cols, rows,
        ),
        out_specs=(rows, rows, cols, cols, rows),
        check_vma=False,
    )
```

time: 158 us -> 137 us (0.87)
  Pallas kernels: 147 us -> 136 us
  local copies, waits for them, and re-layouts: 10.3 us -> 0 us
    pallas_call x1, Pallas kernels: 147 us -> 133 us  [body(): pl.pallas_call(kernel, out_shape=(sds((TOK, D), BF), sds((TOK, D), BF), s...]
    unnamed x19 -> x0, local copies, waits for them, and re-layouts: 7.6 us -> none
    pallas_call x0 -> x1, Pallas kernels: none -> 2.86 us  [body(): pl.pallas_call(hand_over, out_shape=tuple((sds((1, *o.shape), BF) for o i...]
    squeeze x4 -> x0, local copies, waits for them, and re-layouts: 2.72 us -> none  [the longest x1 0.68 us: body(): aff_f[0]]
where the time goes in v2:
time: 137 us; the launch traced here: 136 us
  Pallas kernels  136 us (99%)
    pallas_call x1, Pallas kernels, body(): pl.pallas_call(kernel, out_shape=(sds((TOK, D), BF), sds((TOK, D), BF), s...  133 us
    pallas_call x1, Pallas kernels, body(): pl.pallas_call(hand_over, out_shape=tuple((sds((1, *o.shape), BF) for o i...  2.86 us

profile of v2, /device:TPU:2, one launch (start us, length us, event | category | flops | bytes accessed | tf_op | source)
XLA Modules:
  0.0 136.3 jit_solution(16318714902076936774)
XLA Ops:
  0.6 132.8 %shard_map.191 = (bf16[16,3584]{1,0:T(8,128)(2,1)}, bf16[16,3584]{1,0:T(8,128)(2,1)}, bf16[3584,128]{1,0:T(8,128)(2,1)}, bf16[3584,128]{1,0:T(8,128)(2,1)}, bf16[128,3584]{1,0:T(8,128)(2,1)}) custom-call(bf16[16,3584]{1,0:T(8,128)(2,1)} %fresh.1, bf16[16,3584]{1,0:T(8,128)(2,1)} %bitcast.27, bf16[16,3584]{1,0:T(8,128)(2,1)} %bitcast.28, ...), custom_call_target="tpu_custom_call" | custom-call | tf_op jit(solution)/shard_map/pallas_call | solution.py:587
  133.5 2.9 %shard_map.192 = (bf16[1,16,3584]{2,1,0:T(8,128)(2,1)}, bf16[1,16,3584]{2,1,0:T(8,128)(2,1)}, bf16[1,3584,128]{2,1,0:T(8,128)(2,1)}, bf16[1,3584,128]{2,1,0:T(8,128)(2,1)}, bf16[1,128,3584]{2,1,0:T(8,128)(2,1)}) custom-call(bf16[16,3584]{1,0:T(8,128)(2,1)} %get-tuple-element.10.refs_0_, bf16[16,3584]{1,0:T(8,128)(2,1)} %get-tuple-element.11.refs_1_, ...), custom_call_target="tpu_custom_call" | custom-call | tf_op jit(solution)/shard_map/pallas_call | solution.py:634

commit v3 on v2

--- a/solution.py
+++ b/solution.py
@@ -19,17 +19,25 @@
 CAP = 8
 ROWS_B, GRADS, FRONT = 0, 1, 2
 N_AG = 17
+ORDER = (
+    "enter", "b", "sec", "load", "b", "b", "C", "c", "F", "f", "b", "b", "c", "f", "c", "f",
+    "b", "c", "f", "c", "b", "f", "b", "c", "W", "b", "P0", "c", "P1", "c", "c", "f",
+    "K0", "f", "r", "K1", "r", "f", "f", "H0", "q", "r", "H1", "q", "r", "r", "q", "r",
+    "q", "M", "G0", "r", "q", "r", "q", "G1", "r", "eb", "G2", "q", "G3", "G4", "q", "G5",
+    "save", "ws", "wr", "q", "ef",
+)
 N_RS = 14
 
 
 def kernel(
-    fresh, sent_f, sent_b, turn, saved, gain, ids_f, aff_f, ids_b, aff_b,
+    fresh_in, sent_f, sent_b, turn_in, saved_in, gain_in, ids_f_in, aff_f_in, ids_b_in, aff_b_in,
     w_gate, w_up, w_down, m_gate, m_up, m_down,
     out_f, out_b, o_gate, o_up, o_down,
     tk, g0, g1, packed_y, packed_x, relay, part, core_in, slots_y, relay_back, slots_x,
     tokens, small_in, last_in, pick_y, pick_x, pick_y_t, pick_x_t,
-    wgu, wd, mg, mu, md, dgu_t, hid_t, came_f, came_b,
-    ag_send, ag_recv, rs_send, rs_recv, sec_send, sec_recv, load_sem, save_sem,
+    wgu, wd, mg, mu, md, dgu_t, hid_t, acts, came_f, came_b,
+    fresh, turn, saved, gain, ids_f, aff_f, ids_b, aff_b,
+    ag_send, ag_recv, rs_send, rs_recv, sec_send, sec_recv, load_sem, save_sem, in_sem,
 ):
     sec = lax.axis_index("section")
     ep = lax.axis_index("ep")
@@ -148,25 +156,25 @@
         def same(k, ref, to):
             put(k, ref, ref, to)
 
+        left, right, far = turn4(me, 3), turn4(me, 1), turn4(me, 2)
         same(0, blk(me, z), dev_z)
+        same(1, blk(me, z), dev[0])
+        same(3, blk(me, z), dev[1])
         yield
         got(0, blk(me, 1 - z))
-        left, right, far = turn4(me, 3), turn4(me, 1), turn4(me, 2)
-        same(1, blk(me, 0), dev[0])
-        same(3, blk(me, 1), dev[1])
-        same(2, blk(me, 1), dev[0])
-        same(4, blk(me, 0), dev[1])
-        yield
-        got(1, blk(left, 0))
-        same(5, blk(left, 0), dev[0])
-        got(3, blk(right, 1))
-        same(6, blk(right, 1), dev[1])
-        yield
-        got(2, blk(left, 1))
-        got(4, blk(right, 0))
-        yield
-        got(5, blk(far, 0))
-        got(6, blk(far, 1))
+        same(2, blk(me, 1 - z), dev[0])
+        same(4, blk(me, 1 - z), dev[1])
+        yield
+        got(1, blk(left, z))
+        same(5, blk(left, z), dev[0])
+        got(4, blk(right, 1 - z))
+        same(6, blk(right, 1 - z), dev[1])
+        yield
+        got(2, blk(left, 1 - z))
+        got(3, blk(right, z))
+        yield
+        got(5, blk(far, z))
+        got(6, blk(far, 1 - z))
         pack(u, s)
         if s == 0:
             wide = pl.ds(0, width_of[u])
@@ -396,14 +404,17 @@
     def dot_t(a, b):
         return lax.dot_general(a, b, (((1,), (1,)), ((), ())), preferred_element_type=F32)
 
-    def pre_acts(u, i):
-        a, b = rows_of(u, i)
-        gu = dot(a, wgu[pl.ds(0, W)]) + dot(b, wgu[pl.ds(W, W)])
-        return gu[:, :HID], gu[:, HID:]
+    def pre_acts(u, cc):
+        a, b = rows_of(u, cc)
+        return dot(a, wgu[pl.ds(0, W)]) + dot(b, wgu[pl.ds(W, W)])
+
+    def back_acts(i):
+        acts[i] = pre_acts(ROWS_B, (1 - core, core)[i])
 
     def front_chunk(i):
         cc = (1 - core, core)[i]
-        gate, up = pre_acts(FRONT, cc)
+        both = pre_acts(FRONT, cc)
+        gate, up = both[:, :HID], both[:, HID:]
         hidden = (gate * jax.nn.sigmoid(gate) * up * share_of(FRONT, cc)).astype(BF)
         for s in range(2):
             @pl.loop(0, W // TILE)
@@ -414,7 +425,7 @@
 
     def back_chunk(i):
         cc = (1 - core, core)[i]
-        gate, up = pre_acts(ROWS_B, cc)
+        gate, up = acts[i, :, :HID], acts[i, :, HID:]
         a, b = rows_of(GRADS, cc)
         share = share_of(ROWS_B, cc)
         sig = jax.nn.sigmoid(gate)
@@ -448,119 +459,112 @@
             cot = g[GRADS, :, :, :, :, pl.ds(lo, TILE)].reshape(2 * ROWS, TILE)
             md[:, here] = (md[:, here].astype(F32) + dot(hid_t[...], cot)).astype(BF)
 
-    def step(*gens):
-        for g in gens:
-            next(g, None)
-
-    def finish(*gens):
-        for g in gens:
-            for _ in g:
-                pass
-
-    barrier = pltpu.get_barrier_semaphore()
-    for dev in (dev_z, dev_c, *dev_y, *dev_x, *dev_s):
-        pl.semaphore_signal(barrier, inc=1, device_id=dev, device_id_type=MESH)
-    pl.semaphore_wait(barrier, 8)
-
+    gens = {
+        "b": (ag(ROWS_B, 1), ag(ROWS_B, 0)),
+        "c": (ag(GRADS, 1), ag(GRADS, 0)),
+        "f": (ag(FRONT, 1), ag(FRONT, 0)),
+        "r": (rs(0, 0), rs(0, 1)),
+        "q": (rs(1, 0), rs(1, 1)),
+    }
+    ins = [
+        pltpu.make_async_copy(src, dst, in_sem.at[i])
+        for i, (src, dst) in enumerate((
+            (saved_in, saved), (gain_in, gain), (ids_b_in, ids_b), (aff_b_in, aff_b),
+            (ids_f_in, ids_f), (aff_f_in, aff_f), (turn_in, turn), (fresh_in, fresh),
+        ))
+    ]
     sec_copies = [
         remote(sent_b, came_b, sec_send.at[0], sec_recv.at[0], dev_s[1]),
         remote(sent_f, came_f, sec_send.at[1], sec_recv.at[1], dev_s[0]),
     ]
-    for copy in sec_copies:
-        copy.start()
-    weights_b = weights_of(ids_b, aff_b)
-    place(ROWS_B, norm(saved[...]), weights_b)
-    b = ag(ROWS_B, 0), ag(ROWS_B, 1)
-    c = ag(GRADS, 0), ag(GRADS, 1)
-    f = ag(FRONT, 0), ag(FRONT, 1)
-    r = rs(0, 0), rs(0, 1)
-    q = rs(1, 0), rs(1, 1)
-    step(*b)
-    for copy in loads:
-        copy.start()
-    step(*b)
-    weights_f = weights_of(ids_f, aff_f)
-    step(*b)
-    step(*b)
-    step(*b)
-    sec_copies[0].wait_recv()
-    upstream = jnp.where(sec == 3, turn[...], came_b[...])
-    came_b[...] = upstream
-    place(GRADS, upstream)
-    step(*c)
-    sec_copies[1].wait_recv()
-    front = jnp.where(sec == 0, fresh[...], came_f[...])
-    came_f[...] = front
-    place(FRONT, norm(front), weights_f)
-    step(*b)
-    step(*c)
-    step(*c)
-    step(*b)
-    step(*c)
-    step(*c)
-    step(*f)
-    step(*b)
-    step(*f)
-    step(*c)
-    step(*f)
-    step(*c)
-    step(*f)
-    step(*f)
-    step(*c)
-    finish(*b)
-    finish(*c)
-    for copy in loads[:3]:
-        copy.wait()
-    step(*f)
-    back_chunk(0)
-    step(*f, *r)
-    back_chunk(1)
-    finish(*f)
-    step(*r)
-    front_chunk(0)
-    step(*q, *r)
-    front_chunk(1)
-    step(*r)
-    step(*q)
-    step(*r)
-    step(*r)
-    step(*r)
-    step(*q)
-    finish(*r)
-    for copy in loads[3:]:
-        copy.wait()
-    grad_tiles(0, 0, 7)
-    step(*q)
-    grad_tiles(1, 0, 7)
-    step(*q)
-    step(*q)
-    step(*q)
-    step(*q)
     saves = [
         pltpu.make_async_copy(mg, o_gate, save_sem.at[0]),
         pltpu.make_async_copy(mu, o_up, save_sem.at[1]),
         pltpu.make_async_copy(md, o_down, save_sem.at[2]),
     ]
-    for copy in saves:
-        copy.start()
-
-    values = saved[...].astype(F32)
-    inverse = rinv_of(values)
-    scaled = total_of(0) * gain[...].astype(F32)
-    out_b[...] = (
-        came_b[...].astype(F32)
-        + inverse * scaled
-        - inverse * inverse * inverse * values * jnp.mean(scaled * values, axis=-1, keepdims=True)
-    ).astype(BF)
-    finish(*q)
-    out_f[...] = (came_f[...].astype(F32) + total_of(1)).astype(BF)
+
+    def start_all(copies):
+        for copy in copies:
+            copy.start()
+
+    def wait_all(copies):
+        for copy in copies:
+            copy.wait()
+
+    def enter():
+        start_all(ins)
+        barrier = pltpu.get_barrier_semaphore()
+        for dev in (dev_z, dev_c, *dev_y, *dev_x, *dev_s):
+            pl.semaphore_signal(barrier, inc=1, device_id=dev, device_id_type=MESH)
+        wait_all(ins[:4])
+        place(ROWS_B, norm(saved[...]), weights_of(ids_b, aff_b))
+        pl.semaphore_wait(barrier, 8)
+
+    def place_grads():
+        wait_all(ins[4:])
+        sec_copies[0].wait_recv()
+        upstream = jnp.where(sec == 3, turn[...], came_b[...])
+        came_b[...] = upstream
+        place(GRADS, upstream)
+
+    def place_front():
+        sec_copies[1].wait_recv()
+        front = jnp.where(sec == 0, fresh[...], came_f[...])
+        came_f[...] = front
+        place(FRONT, norm(front), weights_of(ids_f, aff_f))
+
+    def finish_back():
+        values = saved[...].astype(F32)
+        inverse = rinv_of(values)
+        scaled = total_of(0) * gain[...].astype(F32)
+        mean = jnp.mean(scaled * values, axis=-1, keepdims=True)
+        out_b[...] = (
+            came_b[...].astype(F32)
+            + inverse * scaled
+            - inverse * inverse * inverse * values * mean
+        ).astype(BF)
+
+    def finish_front():
+        out_f[...] = (came_f[...].astype(F32) + total_of(1)).astype(BF)
+
+    work = {
+        "enter": enter,
+        "sec": lambda: start_all(sec_copies),
+        "load": lambda: start_all(loads),
+        "C": place_grads,
+        "F": place_front,
+        "W": lambda: wait_all(loads[:3]),
+        "P0": lambda: back_acts(0),
+        "P1": lambda: back_acts(1),
+        "K0": lambda: back_chunk(0),
+        "K1": lambda: back_chunk(1),
+        "H0": lambda: front_chunk(0),
+        "H1": lambda: front_chunk(1),
+        "M": lambda: wait_all(loads[3:]),
+        "G0": lambda: grad_tiles(0, 0, 2),
+        "G1": lambda: grad_tiles(0, 2, 4),
+        "G2": lambda: grad_tiles(0, 4, 7),
+        "G3": lambda: grad_tiles(1, 0, 2),
+        "G4": lambda: grad_tiles(1, 2, 4),
+        "G5": lambda: grad_tiles(1, 4, 7),
+        "save": lambda: start_all(saves),
+        "ws": lambda: [copy.wait_send() for copy in pending],
+        "wr": lambda: [copy.wait_send() for copy in done[:28]],
+        "eb": finish_back,
+        "ef": finish_front,
+    }
+    for token in ORDER:
+        if token[0] in gens:
+            for g in gens[token[0]] if len(token) == 1 else (gens[token[0]][int(token[1])],):
+                next(g, None)
+        else:
+            work[token]()
 
     for copy in sec_copies:
         copy.wait_send()
-    for copy in pending + done:
+    for copy in done[28:]:
         copy.wait_send()
-    for copy in saves:
-        copy.wait()
+    wait_all(saves)
 
 
 def hand_over(*refs):
@@ -590,7 +594,7 @@
             sds((TOK, D), BF), sds((TOK, D), BF),
             sds((D, HID), BF), sds((D, HID), BF), sds((HID, D), BF),
         ),
-        in_specs=[vmem] * 10 + [hbm] * 6,
+        in_specs=[hbm] * 16,
         out_specs=(vmem, vmem, hbm, hbm, hbm),
         scratch_shapes=[
             pltpu.VMEM((2, 3, 4, 2, TOK, W + 128), BF),
@@ -618,11 +622,20 @@
             pltpu.VMEM((HID, D), BF),
             pltpu.VMEM((2 * HID, 2 * ROWS), BF),
             pltpu.VMEM((HID, 2 * ROWS), BF),
+            pltpu.VMEM((2, ROWS, 2 * HID), F32),
             pltpu.VMEM((TOK, D), BF),
             pltpu.VMEM((TOK, D), BF),
+            pltpu.VMEM((TOK, D), BF),
+            pltpu.VMEM((TOK, D), BF),
+            pltpu.VMEM((TOK, D), BF),
+            pltpu.VMEM((1, D), BF),
+            pltpu.VMEM((2, TOK), jnp.int32),
+            pltpu.VMEM((2, TOK), F32),
+            pltpu.VMEM((2, TOK), jnp.int32),
+            pltpu.VMEM((2, TOK), F32),
             dma((6 * N_AG,)), dma((6 * N_AG,)),
             dma((4 * N_RS,)), dma((4 * N_RS,)),
-            dma((2,)), dma((2,)), dma((6,)), dma((3,)),
+            dma((2,)), dma((2,)), dma((6,)), dma((3,)), dma((8,)),
         ],
         compiler_params=pltpu.CompilerParams(
             collective_id=0, has_side_effects=True, vmem_limit_bytes=60 * 2**20

time: 137 us -> 113 us (0.82)
  Pallas kernels: 136 us -> 112 us
    pallas_call x1, Pallas kernels: 133 us -> 110 us  [body(): pl.pallas_call(kernel, out_shape=(sds((TOK, D), BF), sds((TOK, D), BF), s...]
where the time goes in v3:
time: 113 us
  Pallas kernels  112 us (99%)
    pallas_call x1, Pallas kernels, body(): pl.pallas_call(kernel, out_shape=(sds((TOK, D), BF), sds((TOK, D), BF), s...  110 us
    pallas_call x1, Pallas kernels, body(): pl.pallas_call(hand_over, out_shape=tuple((sds((1, *o.shape), BF) for o i...  2.86 us

profile of v3, /device:TPU:2, one launch (start us, length us, event | category | flops | bytes accessed | tf_op | source)
XLA Modules:
  0.0 113.1 jit_solution(7398805028215020857)
XLA Ops:
  0.6 109.6 %shard_map.191 = (bf16[16,3584]{1,0:T(8,128)(2,1)}, bf16[16,3584]{1,0:T(8,128)(2,1)}, bf16[3584,128]{1,0:T(8,128)(2,1)}, bf16[3584,128]{1,0:T(8,128)(2,1)}, bf16[128,3584]{1,0:T(8,128)(2,1)}) custom-call(bf16[16,3584]{1,0:T(8,128)(2,1)} %fresh_in.1, bf16[16,3584]{1,0:T(8,128)(2,1)} %bitcast.27, bf16[16,3584]{1,0:T(8,128)(2,1)} %bitcast.28, ...), custom_call_target="tpu_custom_call" | custom-call | tf_op jit(solution)/shard_map/pallas_call | solution.py:591
  110.2 2.9 %shard_map.192 = (bf16[1,16,3584]{2,1,0:T(8,128)(2,1)}, bf16[1,16,3584]{2,1,0:T(8,128)(2,1)}, bf16[1,3584,128]{2,1,0:T(8,128)(2,1)}, bf16[1,3584,128]{2,1,0:T(8,128)(2,1)}, bf16[1,128,3584]{2,1,0:T(8,128)(2,1)}) custom-call(bf16[16,3584]{1,0:T(8,128)(2,1)} %get-tuple-element.10.refs_0_, bf16[16,3584]{1,0:T(8,128)(2,1)} %get-tuple-element.11.refs_1_, ...), custom_call_target="tpu_custom_call" | custom-call | tf_op jit(solution)/shard_map/pallas_call | solution.py:647

commit v4 on v3

--- a/solution.py
+++ b/solution.py
@@ -18,12 +18,12 @@
 TILE = 256
 CAP = 8
 ROWS_B, GRADS, FRONT = 0, 1, 2
-N_AG = 17
+N_AG = 20
 ORDER = (
     "enter", "b", "sec", "load", "b", "b", "C", "c", "F", "f", "b", "b", "c", "f", "c", "f",
     "b", "c", "f", "c", "b", "f", "b", "c", "W", "b", "P0", "c", "P1", "c", "c", "f",
     "K0", "f", "r", "K1", "r", "f", "f", "H0", "q", "r", "H1", "q", "r", "r", "q", "r",
-    "q", "M", "G0", "r", "q", "r", "q", "G1", "r", "eb", "G2", "q", "G3", "G4", "q", "G5",
+    "q", "M", "G0", "r", "q", "G1", "r", "q", "G2", "r", "eb", "G3", "q", "G4", "q", "G5",
     "save", "ws", "wr", "q", "ef",
 )
 N_RS = 14
@@ -35,7 +35,7 @@
     out_f, out_b, o_gate, o_up, o_down,
     tk, g0, g1, packed_y, packed_x, relay, part, core_in, slots_y, relay_back, slots_x,
     tokens, small_in, last_in, pick_y, pick_x, pick_y_t, pick_x_t,
-    wgu, wd, mg, mu, md, dgu_t, hid_t, acts, came_f, came_b,
+    wgu, wd, mg, mu, md, dgu_t, hid_t, acts, wgu_t, wd_t, came_f, came_b,
     fresh, turn, saved, gain, ids_f, aff_f, ids_b, aff_b,
     ag_send, ag_recv, rs_send, rs_recv, sec_send, sec_recv, load_sem, save_sem, in_sem,
 ):
@@ -157,24 +157,52 @@
             put(k, ref, ref, to)
 
         left, right, far = turn4(me, 3), turn4(me, 1), turn4(me, 2)
-        same(0, blk(me, z), dev_z)
-        same(1, blk(me, z), dev[0])
-        same(3, blk(me, z), dev[1])
-        yield
-        got(0, blk(me, 1 - z))
-        same(2, blk(me, 1 - z), dev[0])
-        same(4, blk(me, 1 - z), dev[1])
-        yield
-        got(1, blk(left, z))
-        same(5, blk(left, z), dev[0])
-        got(4, blk(right, 1 - z))
-        same(6, blk(right, 1 - z), dev[1])
-        yield
-        got(2, blk(left, 1 - z))
-        got(3, blk(right, z))
-        yield
-        got(5, blk(far, z))
-        got(6, blk(far, 1 - z))
+        if u == ROWS_B:
+            same(0, blk(me, z), dev_z)
+            same(1, blk(me, z), dev[0])
+            same(3, blk(me, z), dev[1])
+            yield
+            got(0, blk(me, 1 - z))
+            same(2, blk(me, 1 - z), dev[0])
+            same(4, blk(me, 1 - z), dev[1])
+            yield
+            got(1, blk(left, z))
+            same(5, blk(left, z), dev[0])
+            got(4, blk(right, 1 - z))
+            same(6, blk(right, 1 - z), dev[1])
+            yield
+            got(2, blk(left, 1 - z))
+            got(3, blk(right, z))
+            yield
+            got(5, blk(far, z))
+            got(6, blk(far, 1 - z))
+        else:
+            near = pl.ds(0, W // 2)
+            rest = pl.ds(W // 2, width_of[u] - W // 2)
+
+            def some(i, cols):
+                return tk.at[s, u, i, z, :, cols]
+
+            same(1, blk(me, z), dev[0])
+            same(3, blk(me, z), dev[1])
+            same(0, blk(me, z), dev_z)
+            yield
+            got(1, blk(left, z))
+            same(5, some(left, near), dev[0])
+            got(3, blk(right, z))
+            same(6, some(right, rest), dev[1])
+            same(2, blk(left, z), dev_z)
+            same(4, blk(right, z), dev_z)
+            yield
+            got(5, some(far, near))
+            got(6, some(far, rest))
+            same(17, blk(far, z), dev_z)
+            yield
+            got(0, blk(me, 1 - z))
+            got(2, blk(left, 1 - z))
+            got(4, blk(right, 1 - z))
+            yield
+            got(17, blk(far, 1 - z))
         pack(u, s)
         if s == 0:
             wide = pl.ds(0, width_of[u])
@@ -281,17 +309,21 @@
             got(5, slots_y.at[u, 1, low])
             got(6, slots_y.at[u, 1, high])
         else:
-            put(1, part.at[u, s, core, :, x_far], slots_x.at[u, 0], dev_in)
+            low, high = pl.ds(0, 2), pl.ds(2, 2)
+            put(1, part.at[u, s, core, low, x_far], slots_x.at[u, 0, low], dev_in)
+            put(4, part.at[u, s, core, high, x_far], slots_x.at[u, 0, high], dev_in)
             put(2, part.at[u, s, core, :, x_in], slots_x.at[u, 1], dev_in)
             yield
-            got(1, slots_x.at[u, 0])
-            add_each(part.at[u, s, core, :, x_out], slots_x.at[u, 0])
-            put(3, part.at[u, s, core, :, x_out], slots_x.at[u, 2], dev_out)
+            for k, out, half in ((1, 3, low), (4, 5, high)):
+                got(k, slots_x.at[u, 0, half])
+                add_each(part.at[u, s, core, half, x_out], slots_x.at[u, 0, half], 2)
+                put(out, part.at[u, s, core, half, x_out], slots_x.at[u, 2, half], dev_out)
             yield
             got(2, slots_x.at[u, 1])
-            add_each(part.at[u, s, core, :, x], slots_x.at[u, 1])
-            yield
-            got(3, slots_x.at[u, 2])
+            add_each(part.at[u, s, core, :, x], slots_x.at[u, 1], 4)
+            yield
+            got(3, slots_x.at[u, 2, low])
+            got(5, slots_x.at[u, 2, high])
 
         @pl.loop(0, W // TILE)
         def _(n):
@@ -342,8 +374,8 @@
         yield
         got(13, last_in.at[q])
 
-    def add_each(dst, src):
-        for i in range(4):
+    def add_each(dst, src, count):
+        for i in range(count):
             add_into(dst.at[i], src.at[i])
 
     def total_of(u):
@@ -401,8 +433,14 @@
     def dot(a, b):
         return jnp.dot(a, b, preferred_element_type=F32)
 
-    def dot_t(a, b):
-        return lax.dot_general(a, b, (((1,), (1,)), ((), ())), preferred_element_type=F32)
+    def turn_weights():
+        wait_all(loads[:3])
+
+        @pl.loop(0, D // TILE)
+        def _(n):
+            here = pl.ds(pl.multiple_of(n * TILE, TILE), TILE)
+            wgu_t[:, here] = wgu[here].astype(F32).T.astype(BF)
+            wd_t[here] = wd[:, here].astype(F32).T.astype(BF)
 
     def pre_acts(u, cc):
         a, b = rows_of(u, cc)
@@ -430,7 +468,7 @@
         share = share_of(ROWS_B, cc)
         sig = jax.nn.sigmoid(gate)
         active = gate * sig
-        grad_hidden = (dot_t(a, wd[:, pl.ds(0, W)]) + dot_t(b, wd[:, pl.ds(W, W)])) * share
+        grad_hidden = (dot(a, wd_t[pl.ds(0, W)]) + dot(b, wd_t[pl.ds(W, W)])) * share
         dgate = grad_hidden * up * sig * (1.0 + gate * (1.0 - sig))
         dup = grad_hidden * active
         scaled = active * up * share
@@ -443,7 +481,7 @@
             @pl.loop(0, W // TILE)
             def _(n):
                 lo = pl.multiple_of(n * TILE, TILE)
-                res = dot_t(both, wgu[pl.ds(s * W + lo, TILE)])
+                res = dot(both, wgu_t[:, pl.ds(s * W + lo, TILE)])
                 part[0, s, cc, :, :, :, pl.ds(lo, TILE)] = res.astype(BF).reshape(4, 4, TOK, TILE)
 
     def grad_tiles(s, first, last):
@@ -533,7 +571,7 @@
         "load": lambda: start_all(loads),
         "C": place_grads,
         "F": place_front,
-        "W": lambda: wait_all(loads[:3]),
+        "W": turn_weights,
         "P0": lambda: back_acts(0),
         "P1": lambda: back_acts(1),
         "K0": lambda: back_chunk(0),
@@ -623,6 +661,8 @@
             pltpu.VMEM((2 * HID, 2 * ROWS), BF),
             pltpu.VMEM((HID, 2 * ROWS), BF),
             pltpu.VMEM((2, ROWS, 2 * HID), F32),
+            pltpu.VMEM((2 * HID, D), BF),
+            pltpu.VMEM((D, HID), BF),
             pltpu.VMEM((TOK, D), BF),
             pltpu.VMEM((TOK, D), BF),
             pltpu.VMEM((TOK, D), BF),

time: 113 us -> 111 us (0.982)
  Pallas kernels: 112 us -> 110 us
    pallas_call x1, Pallas kernels: 110 us -> 107 us  [body(): pl.pallas_call(kernel, out_shape=(sds((TOK, D), BF), sds((TOK, D), BF), s...]
where the time goes in v4:
time: 111 us; the launch traced here: 110 us
  Pallas kernels  110 us (99%)
    pallas_call x1, Pallas kernels, body(): pl.pallas_call(kernel, out_shape=(sds((TOK, D), BF), sds((TOK, D), BF), s...  107 us
    pallas_call x1, Pallas kernels, body(): pl.pallas_call(hand_over, out_shape=tuple((sds((1, *o.shape), BF) for o i...  2.86 us

profile of v4, /device:TPU:2, one launch (start us, length us, event | category | flops | bytes accessed | tf_op | source)
XLA Modules:
  0.0 110.3 jit_solution(460448025131181744)
XLA Ops:
  0.6 106.8 %shard_map.191 = (bf16[16,3584]{1,0:T(8,128)(2,1)}, bf16[16,3584]{1,0:T(8,128)(2,1)}, bf16[3584,128]{1,0:T(8,128)(2,1)}, bf16[3584,128]{1,0:T(8,128)(2,1)}, bf16[128,3584]{1,0:T(8,128)(2,1)}) custom-call(bf16[16,3584]{1,0:T(8,128)(2,1)} %fresh_in.1, bf16[16,3584]{1,0:T(8,128)(2,1)} %bitcast.27, bf16[16,3584]{1,0:T(8,128)(2,1)} %bitcast.28, ...), custom_call_target="tpu_custom_call" | custom-call | tf_op jit(solution)/shard_map/pallas_call | solution.py:629
  107.5 2.9 %shard_map.192 = (bf16[1,16,3584]{2,1,0:T(8,128)(2,1)}, bf16[1,16,3584]{2,1,0:T(8,128)(2,1)}, bf16[1,3584,128]{2,1,0:T(8,128)(2,1)}, bf16[1,3584,128]{2,1,0:T(8,128)(2,1)}, bf16[1,128,3584]{2,1,0:T(8,128)(2,1)}) custom-call(bf16[16,3584]{1,0:T(8,128)(2,1)} %get-tuple-element.10.refs_0_, bf16[16,3584]{1,0:T(8,128)(2,1)} %get-tuple-element.11.refs_1_, ...), custom_call_target="tpu_custom_call" | custom-call | tf_op jit(solution)/shard_map/pallas_call | solution.py:687
